TPU v7x, 256 devices: a whole 4x4x8 slice. The times are simulated.
256 devices in a mesh: wave: 32 (over z, y), lev: 8 (over x, core).
Axes of the slice: x: 4, y: 4, z: 8, core: 2. Of those that a mesh axis runs over, the one named last changes fastest.
Arguments:
- fourier: bfloat16 [2560, 128, 4, 128], P('wave', 'lev'), may hold values from -6 to 6
- owner: int32 [64], replicated, may hold values from 0 to 63, each once
- legendre: bfloat16 [64, 2, 640, 1280], P('wave'), may hold values from -0.125 to 0.125
- quad_weights: float32 [1280], replicated, may hold values from 0.5 to 2
- layer_depth: float32 [128], P('lev'), may hold values from 0.05 to 0.3
Outputs:
- fields_out: bfloat16 [2560, 128, 4, 128], P('wave', 'lev')
- geopotential: bfloat16 [2560, 128, 128], P('wave', 'lev')
Inputs may be any that keep to these rules, and one draw needn't show every extreme that they name: owner is a permutation of the slots; slot s lies on index s // 2 of wave.
All inputs are finite; a program needn't handle non-finite values.
Results may differ from a plain program's by a relative error of at most 0.0063.
Values may be sent and summed in bfloat16 or wider, within the bound.
No kernel may reach another device: no remote copies, remote signals or barrier semaphores. Data moves between devices by JAX's collectives and lax.ppermute only.
A program may use at most 64 MiB of HBM per device.

v0:
```python
import jax
import jax.numpy as jnp
from jax import lax
from jax.sharding import PartitionSpec as P

BLOCK = 128


def prefix(part, axis, combine, identity):
    count = lax.axis_size(axis)
    place = lax.axis_index(axis)
    ahead = count - 1 - place
    gathered = lax.all_gather(part, axis)
    state = jnp.zeros_like(part) + jnp.asarray(identity, part.dtype)

    def one(turn, state):
        source = count - 1 - turn
        return combine(state, lax.dynamic_index_in_dim(gathered, source, 0, False))

    return lax.fori_loop(0, ahead, one, state)


def fold_halves(columns, quad_weights):
    values = columns.astype(jnp.float32)
    half_lats = quad_weights.shape[0]
    northern = values[:half_lats]
    southern = values[half_lats:][::-1]
    scaled = quad_weights[:, None]
    return (
        (scaled * (northern + southern)).astype(jnp.bfloat16),
        (scaled * (northern - southern)).astype(jnp.bfloat16),
    )


def legendre_pair(tables, folded, length):
    column_count = folded[0].shape[1]
    halves = []
    for parity in range(2):
        live_rows = (length - parity + 1) // 2
        block_count = (live_rows + BLOCK - 1) // BLOCK
        source = folded[parity]
        parity_table = tables[parity]

        def add_block(
            block_index, totals, parity_table=parity_table, source=source, live_rows=live_rows
        ):
            start = block_index * BLOCK
            rows_here = lax.dynamic_slice_in_dim(parity_table, start, BLOCK, 0)
            spectra = jnp.dot(rows_here, source, preferred_element_type=jnp.float32)
            positions = start + jnp.arange(BLOCK, dtype=jnp.int32)
            spectra = jnp.where((positions < live_rows)[:, None], spectra, 0.0).astype(jnp.bfloat16)
            return totals + lax.dot_general(
                rows_here, spectra, (((0,), (0,)), ((), ())), preferred_element_type=jnp.float32
            )

        zeros_start = jnp.zeros((tables.shape[2], column_count), jnp.float32)
        halves.append(lax.fori_loop(0, block_count, add_block, zeros_start))
    upper = halves[0] + halves[1]
    lower = halves[0] - halves[1]
    return jnp.concatenate([upper, lower[::-1]], axis=0).astype(jnp.bfloat16)


def on_device(fourier, owner, legendre, quad_weights, layer_depth):
    lat_rows, level_count, field_count, doubled = fourier.shape
    waves = doubled // 2
    slots = legendre.shape[0]
    degrees = 2 * legendre.shape[2]
    slot_ids = jnp.arange(waves, dtype=jnp.int32)
    matches = owner[None, :] == slot_ids[:, None]
    wave_of_slot = jnp.sum(jnp.where(matches, slot_ids[None, :], 0), axis=1)
    my_waves = lax.dynamic_slice_in_dim(wave_of_slot, lax.axis_index("wave") * slots, slots, 0)
    lengths = degrees - my_waves * degrees // waves
    unpacked = fourier.reshape(lat_rows, level_count, field_count, 2, waves)
    ordered = jnp.take(unpacked, wave_of_slot, axis=4)
    outgoing = jnp.transpose(ordered, (4, 0, 1, 2, 3)).reshape(
        waves, lat_rows, level_count * field_count * 2
    )
    arrived = lax.all_to_all(outgoing, "wave", split_axis=0, concat_axis=1, tiled=True)
    results = [
        legendre_pair(
            legendre[slot_index],
            fold_halves(arrived[slot_index], quad_weights),
            lengths[slot_index],
        )
        for slot_index in range(slots)
    ]
    stacked = jnp.stack(results, axis=0)
    returned = lax.all_to_all(stacked, "wave", split_axis=1, concat_axis=0, tiled=True)
    restored = jnp.take(returned, owner, axis=0).reshape(
        waves, lat_rows, level_count, field_count, 2
    )
    fields_out = jnp.transpose(restored, (1, 2, 3, 4, 0)).reshape(
        lat_rows, level_count, field_count, doubled
    )
    contrib = layer_depth[None, :, None] * fields_out[:, :, 0, :].astype(jnp.float32)
    inside = jnp.cumsum(contrib[:, ::-1], axis=1)[:, ::-1]
    layer_total = inside[:, 0]
    below = prefix(layer_total, "lev", jnp.add, jnp.zeros_like(layer_total))
    geopotential = (below[:, None, :] + inside - 0.5 * contrib).astype(jnp.bfloat16)
    return (fields_out, geopotential)


def solution(mesh):
    return jax.shard_map(
        on_device,
        mesh=mesh,
        in_specs=(P("wave", "lev", None, None), P(), P("wave", None, None, None), P(), P("lev")),
        out_specs=(P("wave", "lev", None, None), P("wave", "lev", None)),
        check_vma=False,
    )
```

profile of v0, /device:TPU:8, one launch (start us, length us, event | category | flops | bytes accessed | tf_op | source)
XLA Modules:
  0.0 175.3 jit_solution(3042825602504686551)
XLA Ops:
  1.4 3.1 %copy.55 = bf16[80,16,4,128]{0,3,2,1:T(8,128)(2,1)S(1)} copy(bf16[80,16,4,128]{3,2,1,0:T(4,128)(2,1)} %param.15) | data formatting | bytes 2621440 | tf_op args[0]
  4.5 2.7 %copy.56 = bf16[80,16,4,2,64]{0,1,3,2,4:T(8,128)(2,1)} copy(bf16[80,16,4,2,64]{0,4,3,2,1:T(8,128)(2,1)S(1)} %bitcast.88) | data formatting | bytes 2621440 | tf_op jit(solution)/shard_map/reshape | solution.py:73
  7.2 2.5 %gather_fusion = bf16[64,80,16,4,2]{1,2,4,3,0:T(8,128)(2,1)S(1)} fusion(bf16[80,16,4,2,64]{0,1,3,2,4:T(8,128)(2,1)} %copy.56, s32[1024]{0:T(1024)S(1)} %pad_clamp_fusion.1), kind=kCustom, calls=%fused_computation | custom fusion | bytes 2621696 | tf_op jit(solution)/shard_map/jit(_take)/gather | solution.py:74
  11.4 2.7 %copy.58 = bf16[64,80,128]{2,1,0:T(8,128)(2,1)} copy(bf16[64,80,128]{1,0,2:T(8,128)(2,1)S(1)} %bitcast.87) | data formatting | bytes 2621440 | tf_op jit(solution)/shard_map/reshape | solution.py:75
  14.1 11.7 %all-to-all-start = ((bf16[64,80,128]{2,1,0:T(8,128)(2,1)}), bf16[64,80,128]{2,1,0:T(8,128)(2,1)S(1)}, u32[]{:S(2)}, u32[]{:S(2)}) async-start(bf16[64,80,128]{2,1,0:T(8,128)(2,1)} %copy.58), calls=%async_computation | async-start | bytes 2621440 | tf_op jit(solution)/shard_map/all_to_all | solution.py:78
  33.3 5.2 %slice_bitcast_fusion.2 = (bf16[640,1280]{1,0:T(8,128)(2,1)}, bf16[640,1280]{1,0:T(8,128)(2,1)}, bf16[640,1280]{1,0:T(8,128)(2,1)}, bf16[640,1280]{1,0:T(8,128)(2,1)S(1)}) fusion(bf16[2,2,640,1280]{3,2,1,0:T(8,128)(2,1)} %param.17), kind=kLoop, calls=%fused_computation.44 | loop fusion | bytes 13107200 | tf_op jit(solution)/shard_map/squeeze | solution.py:42
  38.5 20.2 %all-to-all-done = bf16[64,80,128]{2,1,0:T(8,128)(2,1)S(1)} async-done(((bf16[64,80,128]{2,1,0:T(8,128)(2,1)}), bf16[64,80,128]{2,1,0:T(8,128)(2,1)S(1)}, u32[]{:S(2)}, u32[]{:S(2)}) %all-to-all-start) | async-done | bytes 1310752 | tf_op jit(solution)/shard_map/all_to_all | solution.py:78
  60.2 3.2 %rev.18 = f32[1280,128]{1,0:T(8,128)} reverse(f32[1280,128]{1,0:T(8,128)S(1)} %bitcast.93), dimensions={0} | reverse | bytes 1310720 | tf_op jit(solution)/shard_map/rev | solution.py:27
  63.4 3.2 %rev.20 = f32[1280,128]{1,0:T(8,128)} reverse(f32[1280,128]{1,0:T(8,128)S(1)} %bitcast.92), dimensions={0} | reverse | bytes 1310720 | tf_op jit(solution)/shard_map/rev | solution.py:27
  66.6 2.9 %fusion.40 = (bf16[1280,128]{1,0:T(8,128)(2,1)S(1)}, bf16[1280,128]{1,0:T(8,128)(2,1)}, bf16[1280,128]{1,0:T(8,128)(2,1)S(1)}, bf16[1280,128]{1,0:T(8,128)(2,1)}) fusion(f32[1280,128]{1,0:T(8,128)} %rev.18, f32[1,16,80,128]{3,2,0,1:T(8,128)} %get-tuple-element.271, f32[1280]{0:T(1024)S(1)} %copy-done.2, f32[1280,128]{1,0:T(8,128)} %rev.20, ...), kind=kLoop, calls=%fused_computation.61 | loop fusion | flops 1966080 | bytes 3937280 | tf_op jit(solution)/shard_map/convert_element_type | solution.py:31
  71.2 1.7 while.52
  71.3 1.7 convolution_add_fusion.8
  74.6 8.6 %while.55 = (s32[]{:T(128)}, f32[1280,128]{1,0:T(8,128)S(1)}, s32[]{:T(128)}, bf16[640,1280]{1,0:T(8,128)(2,1)}, s32[]{:T(128)}, /*index=5*/bf16[1280,128]{1,0:T...) while((s32[]{:T(128)}, f32[1280,128]{1,0:T(8,128)S(1)}, s32[]{:T(128)}, bf16[640,1280]{1,0:T(8,128)(2,1)}, ...), condition=%wide.region_8.9_spmd, body=%wide.region_7.8_spmd.sunk | while | flops 84082952 | bytes 2295195 | solution.py:57
  74.6 1.7 convolution_add_fusion.11
  76.4 1.7 convolution_add_fusion.11
  78.1 1.7 convolution_add_fusion.11
  83.3 2.9 %while.54 = (s32[]{:T(128)}, f32[1280,128]{1,0:T(8,128)S(1)}, s32[]{:T(128)}, bf16[640,1280]{1,0:T(8,128)(2,1)S(1)}, s32[]{:T(128)}, /*index=5*/bf16[1280,128]{1...) while((s32[]{:T(128)}, f32[1280,128]{1,0:T(8,128)S(1)}, s32[]{:T(128)}, ...), condition=%wide.region_6.7_spmd, body=%wide.region_5.6_spmd.sunk | while | flops 84082952 | bytes 2295579 | solution.py:57
  87.9 11.6 %copy.59 = bf16[2,2560,128]{2,0,1:T(2,128)(2,1)} copy(bf16[2,2560,128]{2,1,0:T(8,128)(2,1)S(1)} %maximum_maximum_fusion) | data formatting | bytes 2621440 | tf_op jit(solution)/shard_map/stack | solution.py:87
  99.6 17.0 %all-to-all-start.1 = ((bf16[2,2560,128]{2,0,1:T(2,128)(2,1)}), bf16[2,2560,128]{2,0,1:T(2,128)(2,1)S(1)}, u32[]{:S(2)}, u32[]{:S(2)}) async-start(bf16[2,2560,128]{2,0,1:T(2,128)(2,1)} %copy.59), calls=%async_computation.1 | async-start | bytes 2621440 | tf_op jit(solution)/shard_map/all_to_all | solution.py:88
  116.6 32.9 %all-to-all-done.1 = bf16[2,2560,128]{2,0,1:T(2,128)(2,1)S(1)} async-done(((bf16[2,2560,128]{2,0,1:T(2,128)(2,1)}), bf16[2,2560,128]{2,0,1:T(2,128)(2,1)S(1)}, u32[]{:S(2)}, u32[]{:S(2)}) %all-to-all-start.1) | async-done | bytes 1310752 | tf_op jit(solution)/shard_map/all_to_all | solution.py:88
  150.5 2.7 %copy.62 = bf16[64,80,128]{1,0,2:T(8,128)(2,1)S(1)} copy(bf16[64,80,128]{2,1,0:T(8,128)(2,1)S(1)} %gather_fusion.1) | data formatting | bytes 2621440 | tf_op jit(solution)/shard_map/jit(_take)/gather | solution.py:89
  153.2 2.0 %fusion.32 = bf16[80,16,4,2,64]{0,1,3,2,4:T(8,128)(2,1)S(1)} fusion(bf16[64,80,16,4,2]{1,0,4,3,2:T(8,128)(2,1)S(1)} %bitcast.86, pred[64]{0:T(512)(128)(4,1)S(1)} %compare_and_fusion.1), kind=kLoop, calls=%fused_computation.40 | loop fusion | flops 655360 | bytes 2621504 | tf_op jit(solution)/shard_map/transpose | solution.py:92
  156.6 2.4 %copy.66 = bf16[80,16,4,128]{3,2,1,0:T(4,128)(2,1)} copy(bf16[80,16,4,128]{0,3,2,1:T(8,128)(2,1)S(1)} %bitcast.85) | data formatting | bytes 2621440
  160.7 13.3 %all-gather = f32[640,1,128]{2,0,1:T(8,128)S(1)} all-gather(f32[80,1,128]{2,0,1:T(8,128)S(1)} %slice.96), channel_id=2, replica_groups=mesh['wave'=32,'lev'=8] {'lev'}, dimensions={0}, use_global_device_ids=true | all-gather | bytes 368640 | tf_op jit(solution)/shard_map/all_gather | solution.py:13
  (76 shorter events, 22.7 us)
Async XLA Ops:
  14.1 44.6 %all-to-all-start = ((bf16[64,80,128]{2,1,0:T(8,128)(2,1)}), bf16[64,80,128]{2,1,0:T(8,128)(2,1)S(1)}, u32[]{:S(2)}, u32[]{:S(2)}) async-start(bf16[64,80,128]{2,1,0:T(8,128)(2,1)} %copy.58), calls=%async_computation | async-start | bytes 2621440 | tf_op jit(solution)/shard_map/all_to_all | solution.py:78
  60.2 6.4 %copy-start.2 = (f32[1280]{0:T(1024)S(1)}, f32[1280]{0:T(1024)}, u32[]{:S(2)}) copy-start(f32[1280]{0:T(1024)} %param.18) | copy-start | bytes 15364
  86.2 1.0 copy-start.1
  86.3 1.6 copy-start
  99.6 17.0 %copy-start.4 = (s32[64]{0:T(128)S(1)}, s32[64]{0:T(128)}, u32[]{:S(2)}) copy-start(s32[64]{0:T(128)} %param.16) | copy-start | bytes 772
  99.6 49.9 %all-to-all-start.1 = ((bf16[2,2560,128]{2,0,1:T(2,128)(2,1)}), bf16[2,2560,128]{2,0,1:T(2,128)(2,1)S(1)}, u32[]{:S(2)}, u32[]{:S(2)}) async-start(bf16[2,2560,128]{2,0,1:T(2,128)(2,1)} %copy.59), calls=%async_computation.1 | async-start | bytes 2621440 | tf_op jit(solution)/shard_map/all_to_all | solution.py:88
  156.6 2.7 %copy-start.3 = (f32[16]{0:T(128)S(1)}, f32[16]{0:T(128)}, u32[]{:S(2)}) copy-start(f32[16]{0:T(128)} %param.19) | copy-start | bytes 196
where the time goes:
time: 177 us; the launch traced here: 175 us
  waiting for transfers between devices  53 us (30%)
  local copies, waits for them, and re-layouts  47.8 us (27%)
  starting transfers between devices  28.7 us (16%)
  matrix products  14.1 us (8%)
  blocking collectives  13.3 us (8%)
  other arithmetic  9.72 us (5%)
  between operations  7.77 us (4%)
    all_to_all x1, waiting for transfers between devices, on_device(): lax.all_to_all(stacked, 'wave', split_axis=1, concat_axis=0, tiled=True)  32.9 us
    all_to_all x1, waiting for transfers between devices, on_device(): lax.all_to_all(outgoing, 'wave', split_axis=0, concat_axis=1, tiled=True)  20.2 us
    all_to_all x1, starting transfers between devices, on_device(): lax.all_to_all(stacked, 'wave', split_axis=1, concat_axis=0, tiled=True)  17 us
    dot_general x12, matrix products, add_block(): lax.dot_general(rows_here, spectra, (((0,), (0,)), ((), ())), preferred_e...  14.1 us
    all_gather x1, blocking collectives, prefix(): gathered = lax.all_gather(part, axis)  13.3 us
    all_to_all x1, starting transfers between devices, on_device(): lax.all_to_all(outgoing, 'wave', split_axis=0, concat_axis=1, tiled=True)  11.7 us
    another operation x1, local copies, waits for them, and re-layouts, on_device(): stacked = jnp.stack(results, axis=0)  11.6 us
    unnamed x14, local copies, waits for them, and re-layouts  7.34 us
  transfers between devices with their start and end apart: 2, of which 2 were waited for; matrix products, arithmetic and copies ran while one was open for 3% of the time, Pallas kernels for 0%

commit v1 on v0

v1 whole, which is shorter than its diff:
```python
import jax
import jax.numpy as jnp
from jax import lax
from jax.experimental import pallas as pl
from jax.experimental.pallas import tpu as pltpu
from jax.sharding import PartitionSpec as P

F32 = jnp.float32
BF16 = jnp.bfloat16
NT = (((1,), (1,)), ((), ()))
NN = (((1,), (0,)), ((), ()))
VMEM = pl.BlockSpec(memory_space=pltpu.VMEM)
SMEM = pl.BlockSpec(memory_space=pltpu.SMEM)
ANY = pl.BlockSpec(memory_space=pl.ANY)


def dot(a, b, dims):
    return lax.dot_general(a, b, dims, preferred_element_type=F32)


def identity(size):
    rows = lax.broadcasted_iota(jnp.int32, (size, size), 0)
    cols = lax.broadcasted_iota(jnp.int32, (size, size), 1)
    return jnp.where(rows == cols, 1.0, 0.0).astype(BF16)


def regroup(first, second):
    lanes = first.shape[1]
    half = lanes // 2
    low = lax.broadcasted_iota(jnp.int32, first.shape, 1) < half
    return (
        jnp.where(low, first, pltpu.roll(second, half, 1)),
        jnp.where(low, pltpu.roll(first, half, 1), second),
    )


def pack_kernel(owner_ref, flip_ref, x_ref, out_ref, spread):
    waves, lat_rows, lanes = out_ref.shape
    eye = identity(lanes)
    flip = flip_ref[0]

    def pair(turn, _):
        rows = x_ref[pl.ds(turn * lanes, lanes), :]
        turned = dot(eye, rows, NT)
        tiles = regroup(turned[:waves], turned[waves:])
        for step, tile in enumerate(tiles):
            lat = 2 * turn + step
            place = jnp.where(flip > 0, lat_rows - 1 - lat, lat)
            spread[pl.ds(place, waves, stride=lat_rows), :] = tile
        return 0

    lax.fori_loop(0, lat_rows // 2, pair, 0, unroll=4)

    def slot(wave, _):
        out_ref[owner_ref[wave]] = spread[pl.ds(wave * lat_rows, lat_rows), :].astype(BF16)
        return 0

    lax.fori_loop(0, waves, slot, 0, unroll=4)


def pack(x, owner, flip):
    lat_rows, level_count, field_count, lanes = x.shape
    waves = lanes // 2
    return pl.pallas_call(
        pack_kernel,
        out_shape=jax.ShapeDtypeStruct((waves, lat_rows, lanes), BF16),
        in_specs=[SMEM, SMEM, VMEM],
        out_specs=VMEM,
        scratch_shapes=[pltpu.VMEM((waves * lat_rows, lanes), F32)],
        name="pack",
    )(owner, flip, x.reshape(lat_rows * level_count * field_count, lanes))


def legendre_kernel(length_ref, weight_ref, x_ref, table_hbm, out_ref, table, folded, sems):
    blocks, slots, lat_rows, lanes = x_ref.shape
    half_blocks = blocks // 2
    rows, half_lats = table.shape[2:]
    copies = []
    for slot in range(slots):
        for parity in range(2):
            copy = pltpu.make_async_copy(
                table_hbm.at[slot, parity], table.at[slot, parity], sems.at[slot, parity]
            )
            copy.start()
            copies.append(copy)
    for slot in range(slots):
        for block in range(half_blocks):
            span = pl.ds(block * lat_rows, lat_rows)
            north = x_ref[block, slot].astype(F32)
            south = x_ref[blocks - 1 - block, slot].astype(F32)
            weight = weight_ref[span, :]
            folded[0, span, :] = (weight * (north + south)).astype(BF16)
            folded[1, span, :] = (weight * (north - south)).astype(BF16)
        parts = []
        for parity in range(2):
            copies[slot * 2 + parity].wait()
            spectra = dot(table[slot, parity], folded[parity], NN)
            degree = 2 * lax.broadcasted_iota(jnp.int32, spectra.shape, 0) + parity
            spectra = jnp.where(degree < length_ref[slot], spectra, 0.0)
            parts.append(dot(spectra.T.astype(BF16), table[slot, parity], NN))
        upper = (parts[0] + parts[1]).T.astype(BF16)
        lower = (parts[0] - parts[1]).T.astype(BF16)
        for block in range(half_blocks):
            span = slice(block * lat_rows, (block + 1) * lat_rows)
            out_ref[block, slot] = upper[span]
            out_ref[blocks - 1 - block, slot] = lower[span]


def legendre_pair(x, table, weight, length):
    half_lats, lanes = weight.shape
    return pl.pallas_call(
        legendre_kernel,
        out_shape=jax.ShapeDtypeStruct(x.shape, BF16),
        in_specs=[SMEM, VMEM, VMEM, ANY],
        out_specs=VMEM,
        scratch_shapes=[
            pltpu.VMEM(table.shape, BF16),
            pltpu.VMEM((2, half_lats, lanes), BF16),
            pltpu.SemaphoreType.DMA((table.shape[0], 2)),
        ],
        name="legendre",
    )(length, weight, x, table)


def unpack_kernel(owner_ref, flip_ref, mix_ref, x_ref, out_ref, geo_ref, total_ref, spread):
    waves, lat_rows, lanes = x_ref.shape
    levels = geo_ref.shape[1]
    flip = flip_ref[0]

    def slot(wave, _):
        spread[pl.ds(wave * lat_rows, lat_rows), :] = x_ref[owner_ref[wave]].astype(F32)
        return 0

    lax.fori_loop(0, waves, slot, 0, unroll=4)
    mix = mix_ref[...]

    def pair(turn, _):
        tiles = []
        for step in range(2):
            lat = 2 * turn + step
            place = jnp.where(flip > 0, lat_rows - 1 - lat, lat)
            tiles.append(spread[pl.ds(place, waves, stride=lat_rows), :])
        rows = jnp.concatenate(tiles, axis=0).astype(BF16)
        turned = dot(mix, rows, NT)
        for step, tile in enumerate(regroup(turned[:waves], turned[waves : 2 * waves])):
            out_ref[2 * turn + step] = tile.astype(BF16)
        sums = turned[lanes : lanes + 48] + turned[lanes + 48 : lanes + 96]
        for step, tile in enumerate(regroup(sums[:24], sums[24:])):
            geo_ref[2 * turn + step] = tile[:levels]
            total_ref[pl.ds(2 * turn + step, 1), :] = tile[levels : levels + 1]
        return 0

    lax.fori_loop(0, lat_rows // 2, pair, 0, unroll=4)


def unpack(x, owner, flip, mix, levels):
    waves, lat_rows, lanes = x.shape
    return pl.pallas_call(
        unpack_kernel,
        out_shape=(
            jax.ShapeDtypeStruct((lat_rows, waves, lanes), BF16),
            jax.ShapeDtypeStruct((lat_rows, levels, lanes), F32),
            jax.ShapeDtypeStruct((lat_rows, lanes), F32),
        ),
        in_specs=[SMEM, SMEM, VMEM, VMEM],
        out_specs=(VMEM, VMEM, VMEM),
        scratch_shapes=[pltpu.VMEM((waves * lat_rows, lanes), F32)],
        name="unpack",
    )(owner, flip, mix, x)


def mixing(layer_depth, field_count):
    levels = layer_depth.shape[0]
    columns = levels * field_count
    to = jnp.arange(24)[:, None]
    column = jnp.arange(columns)[None, :]
    level = column // field_count
    share = jnp.where(to == level, 0.5, jnp.where(to < level, 1.0, 0.0))
    share = jnp.where(to == levels, 1.0, jnp.where(to > levels, 0.0, share))
    share = jnp.where(column % field_count == 0, share, 0.0)
    weight = share * jnp.repeat(layer_depth, field_count)[None, :]
    high = weight.astype(BF16)
    low = (weight - high.astype(F32)).astype(BF16)
    blank = jnp.zeros_like(high)
    both = [
        jnp.concatenate(pieces, axis=1)
        for pieces in ((high, blank), (blank, high), (low, blank), (blank, low))
    ]
    return jnp.concatenate([jnp.eye(2 * columns, dtype=BF16)] + both, axis=0)


def on_device(fourier, owner, legendre, quad_weights, layer_depth):
    lat_rows, level_count, field_count, doubled = fourier.shape
    waves = doubled // 2
    slots = legendre.shape[0]
    degrees = 2 * legendre.shape[2]
    blocks = waves // slots
    place = lax.axis_index("wave")
    flip = (place >= blocks // 2).astype(jnp.int32).reshape(1)
    mine = place * slots + jnp.arange(slots, dtype=jnp.int32)
    wave_ids = jnp.arange(waves, dtype=jnp.int32)
    my_waves = jnp.sum(jnp.where(owner[None, :] == mine[:, None], wave_ids[None, :], 0), axis=1)
    lengths = degrees - my_waves * degrees // waves
    weight = jnp.broadcast_to(quad_weights[:, None], (quad_weights.shape[0], doubled))
    mix = mixing(layer_depth, field_count)

    outgoing = pack(fourier, owner, flip)
    arrived = lax.all_to_all(outgoing, "wave", split_axis=0, concat_axis=0, tiled=True)
    arrived = arrived.reshape(blocks, slots, lat_rows, doubled)
    results = legendre_pair(arrived, legendre, weight, lengths)
    results = results.reshape(waves, lat_rows, doubled)
    returned = lax.all_to_all(results, "wave", split_axis=0, concat_axis=0, tiled=True)
    fields, inside, total = unpack(returned, owner, flip, mix, level_count)
    fields_out = fields.reshape(fourier.shape)
    gathered = lax.all_gather(total, "lev")
    lev = lax.axis_index("lev")
    later = jnp.arange(gathered.shape[0], dtype=jnp.int32) > lev
    below = jnp.sum(jnp.where(later[:, None, None], gathered, 0.0), axis=0)
    geopotential = (below[:, None, :] + inside).astype(BF16)
    return (fields_out, geopotential)


def solution(mesh):
    return jax.shard_map(
        on_device,
        mesh=mesh,
        in_specs=(P("wave", "lev", None, None), P(), P("wave", None, None, None), P(), P("lev")),
        out_specs=(P("wave", "lev", None, None), P("wave", "lev", None)),
        check_vma=False,
    )
```

time: 177 us -> 127 us (0.72)
  local copies, waits for them, and re-layouts: 47.8 us -> 2.76 us
  Pallas kernels: 0 us -> 23.7 us
  matrix products: 14.1 us -> 0 us
  waiting for transfers between devices: 53 us -> 64.3 us
  starting transfers between devices: 28.7 us -> 18.2 us
  between operations: 7.77 us -> 0.75 us
  other arithmetic: 9.72 us -> 2.81 us
    pallas_call x0 -> x3, Pallas kernels: none -> 23.7 us  [the longest x1 10.7 us: legendre_pair(): pl.pallas_call(legendre_kernel, out_shape=jax.ShapeDtypeStruct(x.shape, B...]
    dot_general x12 -> x0, matrix products: 14.1 us -> none  [add_block(): lax.dot_general(rows_here, spectra, (((0,), (0,)), ((), ())), preferred_e...]
    another operation x5 -> x0, local copies, waits for them, and re-layouts: 11.8 us -> none  [the longest x1 11.6 us: on_device(): stacked = jnp.stack(results, axis=0)]
    all_to_all x2, waiting for transfers between devices: 53 us -> 64.3 us  [the longest x1 32.2 us: on_device(): lax.all_to_all(outgoing, 'wave', split_axis=0, concat_axis=0, tiled=True)]
    all_to_all x2, starting transfers between devices: 28.7 us -> 18.2 us  [the longest x1 11.8 us: on_device(): lax.all_to_all(outgoing, 'wave', split_axis=0, concat_axis=0, tiled=True)]
    rev x5 -> x0, local copies, waits for them, and re-layouts: 7.09 us -> none  [the longest x2 6.39 us: fold_halves(): southern = values[half_lats:][::-1]]
    unnamed x14 -> x15, local copies, waits for them, and re-layouts: 7.34 us -> 1.2 us
    gather x3 -> x0, local copies, waits for them, and re-layouts: 6 us -> none  [the longest x2 3.46 us: on_device(): jnp.take(returned, owner, axis=0)]
  transfers between devices with their start and end apart: 2 -> 2, of which waited for: 2 -> 2; matrix products, arithmetic and copies ran while one was open for 3% -> 1% of each run, Pallas kernels for 0% -> 0%
where the time goes in v1:
time: 127 us; the launch traced here: 126 us
  waiting for transfers between devices  64.3 us (51%)
  Pallas kernels  23.7 us (19%)
  starting transfers between devices  18.2 us (14%)
  blocking collectives  13.4 us (11%)
  other arithmetic  2.81 us (2%)
  local copies, waits for them, and re-layouts  2.76 us (2%)
    all_to_all x1, waiting for transfers between devices, on_device(): lax.all_to_all(outgoing, 'wave', split_axis=0, concat_axis=0, tiled=True)  32.2 us
    all_to_all x1, waiting for transfers between devices, on_device(): lax.all_to_all(results, 'wave', split_axis=0, concat_axis=0, tiled=True)  32.1 us
    all_gather x1, blocking collectives, on_device(): gathered = lax.all_gather(total, 'lev')  13.4 us
    all_to_all x1, starting transfers between devices, on_device(): lax.all_to_all(outgoing, 'wave', split_axis=0, concat_axis=0, tiled=True)  11.8 us
    pallas_call x1, Pallas kernels, legendre_pair(): pl.pallas_call(legendre_kernel, out_shape=jax.ShapeDtypeStruct(x.shape, B...  10.7 us
    pallas_call x1, Pallas kernels, unpack(): pl.pallas_call(unpack_kernel, out_shape=(jax.ShapeDtypeStruct((lat_rows,...  6.79 us
    all_to_all x1, starting transfers between devices, on_device(): lax.all_to_all(results, 'wave', split_axis=0, concat_axis=0, tiled=True)  6.35 us
    pallas_call x1, Pallas kernels, pack(): pl.pallas_call(pack_kernel, out_shape=jax.ShapeDtypeStruct((waves, lat_ro...  6.29 us
  transfers between devices with their start and end apart: 2, of which 2 were waited for; matrix products, arithmetic and copies ran while one was open for 1% of the time, Pallas kernels for 0%

profile of v1, /device:TPU:8, one launch (start us, length us, event | category | flops | bytes accessed | tf_op | source)
XLA Modules:
  0.0 126.0 jit_solution(2872667604091083311)
XLA Ops:
  0.6 6.3 %pack.1 = bf16[64,80,128]{2,1,0:T(8,128)(2,1)} custom-call(s32[64]{0:T(128)} %owner_ref.3, s32[1]{0:T(128)} %bitcast.flip_ref, bf16[5120,128]{1,0:T(8,128)(2,1)} %bitcast.8), custom_call_target="tpu_custom_call" | custom-call | tf_op jit(solution)/shard_map/pack/pallas_call | solution.py:64
  6.9 11.8 %all-to-all-start = ((bf16[64,80,128]{2,1,0:T(8,128)(2,1)}), bf16[64,80,128]{2,1,0:T(8,128)(2,1)S(1)}, u32[]{:S(2)}, u32[]{:S(2)}) async-start(bf16[64,80,128]{2,1,0:T(8,128)(2,1)} %pack.1), calls=%async_computation | async-start | bytes 2621440 | tf_op jit(solution)/shard_map/all_to_all | solution.py:208
  18.8 0.0 copy-done.4
  18.8 0.2 fusion.3
  19.0 0.5 fusion.5.length_ref
  19.5 32.2 %all-to-all-done = bf16[64,80,128]{2,1,0:T(8,128)(2,1)S(1)} async-done(((bf16[64,80,128]{2,1,0:T(8,128)(2,1)}), bf16[64,80,128]{2,1,0:T(8,128)(2,1)S(1)}, u32[]{:S(2)}, u32[]{:S(2)}) %all-to-all-start) | async-done | bytes 1310752 | tf_op jit(solution)/shard_map/all_to_all | solution.py:208
  51.7 0.0 copy-done.3
  51.7 1.3 %broadcast_in_dim.88.weight_ref = f32[1280,128]{1,0:T(8,128)} broadcast(f32[1280]{0:T(1024)S(1)} %copy-done.3), dimensions={0} | broadcast | bytes 660480 | tf_op jit(solution)/shard_map/broadcast_in_dim | solution.py:204
  53.0 0.0 copy-done
  53.0 10.7 %legendre.1 = bf16[32,2,80,128]{3,2,1,0:T(8,128)(2,1)} custom-call(s32[2]{0:T(128)} %fusion.5.length_ref, f32[1280,128]{1,0:T(8,128)} %broadcast_in_dim.88.weight_ref, bf16[32,2,80,128]{3,2,1,0:T(8,128)(2,1)} %bitcast.7, bf16[2,2,640,1280]{3,2,1,0:T(8,128)(2,1)} %table_hbm.1), custom_call_target="tpu_custom_call" | custom-call | tf_op jit(solution)/shard_map/legendre/pallas_call | solution.py:111
  63.7 0.0 copy-start.5
  63.7 6.3 %all-to-all-start.1 = ((bf16[64,80,128]{2,1,0:T(8,128)(2,1)}), bf16[64,80,128]{2,1,0:T(8,128)(2,1)S(1)}, u32[]{:S(2)}, u32[]{:S(2)}) async-start(bf16[64,80,128]{2,1,0:T(8,128)(2,1)} %bitcast.6), calls=%async_computation.1 | async-start | bytes 2621440 | tf_op jit(solution)/shard_map/all_to_all | solution.py:212
  70.1 0.1 broadcast_in_dim.85
  70.1 0.1 mul.16
  70.3 0.1 subtract_convert_fusion
  70.4 0.1 constant_dynamic-update-slice_fusion.2
  70.5 0.1 constant_dynamic-update-slice_fusion.mix_ref
  70.6 32.1 %all-to-all-done.1.x_ref = bf16[64,80,128]{2,1,0:T(8,128)(2,1)S(1)} async-done(((bf16[64,80,128]{2,1,0:T(8,128)(2,1)}), bf16[64,80,128]{2,1,0:T(8,128)(2,1)S(1)}, u32[]{:S(2)}, u32[]{:S(2)}) %all-to-all-start.1) | async-done | bytes 1310752 | tf_op jit(solution)/shard_map/all_to_all | solution.py:212
  102.7 0.0 copy-done.2
  102.7 1.1 copy-done.1
  103.7 6.8 %unpack.1 = (bf16[80,64,128]{2,1,0:T(8,128)(2,1)}, f32[80,16,128]{2,1,0:T(8,128)}, f32[80,128]{1,0:T(8,128)}) custom-call(s32[64]{0:T(128)} %owner_ref.3, s32[1]{0:T(128)} %bitcast.flip_ref, bf16[224,128]{1,0:T(8,128)(2,1)} %copy-done.2, bf16[64,80,128]{2,1,0:T(8,128)(2,1)} %copy-done.1), custom_call_target="tpu_custom_call" | custom-call | tf_op jit(solution)/shard_map/unpack/pallas_call | solution.py:158
  110.5 13.4 %all-gather = f32[640,128]{1,0:T(8,128)S(1)} all-gather(f32[80,128]{1,0:T(8,128)} %get-tuple-element.6), channel_id=2, replica_groups=mesh['wave'=32,'lev'=8] {'lev'}, dimensions={0}, use_global_device_ids=true | all-gather | bytes 368640 | tf_op jit(solution)/shard_map/all_gather | solution.py:215
  124.0 0.1 select_reduce_fusion
  124.1 1.9 %add_convert_fusion = bf16[80,16,128]{2,1,0:T(8,128)(2,1)} fusion(f32[80,16,128]{2,1,0:T(8,128)} %get-tuple-element.7, f32[80,128]{1,0:T(8,128)S(1)} %select_reduce_fusion), kind=kLoop, calls=%fused_computation | loop fusion | flops 327680 | bytes 1024000 | tf_op jit(solution)/shard_map/convert_element_type | solution.py:219
  (14 shorter events, 0.1 us)
Async XLA Ops:
  6.9 11.9 %copy-start.4 = (s32[64]{0:T(128)S(1)}, s32[64]{0:T(128)}, u32[]{:S(2)}) copy-start(s32[64]{0:T(128)} %owner_ref.3) | copy-start | bytes 772
  6.9 44.8 %copy-start.3 = (f32[1280]{0:T(1024)S(1)}, f32[1280]{0:T(1024)}, u32[]{:S(2)}) copy-start(f32[1280]{0:T(1024)} %param.8) | copy-start | bytes 15364
  6.9 44.7 %all-to-all-start = ((bf16[64,80,128]{2,1,0:T(8,128)(2,1)}), bf16[64,80,128]{2,1,0:T(8,128)(2,1)S(1)}, u32[]{:S(2)}, u32[]{:S(2)}) async-start(bf16[64,80,128]{2,1,0:T(8,128)(2,1)} %pack.1), calls=%async_computation | async-start | bytes 2621440 | tf_op jit(solution)/shard_map/all_to_all | solution.py:208
  51.7 1.3 %copy-start = (bf16[64,80,128]{2,1,0:T(8,128)(2,1)}, bf16[64,80,128]{2,1,0:T(8,128)(2,1)S(1)}, u32[]{:S(2)}) copy-start(bf16[64,80,128]{2,1,0:T(8,128)(2,1)S(1)} %all-to-all-done) | copy-start | bytes 3932164
  63.7 6.4 %copy-start.5 = (f32[16]{0:T(128)S(1)}, f32[16]{0:T(128)}, u32[]{:S(2)}) copy-start(f32[16]{0:T(128)} %param.9) | copy-start | bytes 196
  63.7 39.0 %all-to-all-start.1 = ((bf16[64,80,128]{2,1,0:T(8,128)(2,1)}), bf16[64,80,128]{2,1,0:T(8,128)(2,1)S(1)}, u32[]{:S(2)}, u32[]{:S(2)}) async-start(bf16[64,80,128]{2,1,0:T(8,128)(2,1)} %bitcast.6), calls=%async_computation.1 | async-start | bytes 2621440 | tf_op jit(solution)/shard_map/all_to_all | solution.py:212
  70.6 32.1 %copy-start.2 = (bf16[224,128]{1,0:T(8,128)(2,1)}, bf16[224,128]{1,0:T(8,128)(2,1)S(1)}, u32[]{:S(2)}) copy-start(bf16[224,128]{1,0:T(8,128)(2,1)S(1)} %constant_dynamic-update-slice_fusion.mix_ref) | copy-start | bytes 172036
  102.7 1.1 copy-start.1

commit v2 on v1

v2 whole, which is shorter than its diff:
```python
import jax
import jax.numpy as jnp
from jax import lax
from jax.experimental import pallas as pl
from jax.experimental.pallas import tpu as pltpu
from jax.sharding import PartitionSpec as P

F32 = jnp.float32
BF16 = jnp.bfloat16
MIB = 1 << 20
PAD = 8
NT = (((1,), (1,)), ((), ()))
NN = (((1,), (0,)), ((), ()))
VMEM = pl.BlockSpec(memory_space=pltpu.VMEM)
SMEM = pl.BlockSpec(memory_space=pltpu.SMEM)
ANY = pl.BlockSpec(memory_space=pl.ANY)
HBM = pl.BlockSpec(memory_space=pltpu.HBM)


def dot(a, b, dims):
    return lax.dot_general(a, b, dims, preferred_element_type=F32)


def identity(size):
    rows = lax.broadcasted_iota(jnp.int32, (size, size), 0)
    cols = lax.broadcasted_iota(jnp.int32, (size, size), 1)
    return jnp.where(rows == cols, 1.0, 0.0).astype(BF16)


def regroup(first, second):
    half = first.shape[1] // 2
    return jnp.concatenate(
        [
            jnp.concatenate([first[:, :half], second[:, :half]], axis=1),
            jnp.concatenate([first[:, half:], second[:, half:]], axis=1),
        ],
        axis=0,
    )


def pack_kernel(owner_ref, flip_ref, x_ref, out_ref, spread):
    waves, lat_rows, lanes = out_ref.shape
    eye = identity(lanes)
    flip = flip_ref[0]
    for turn in range(lat_rows // 4):
        rows = [x_ref[lat * waves : (lat + 1) * waves, :] for lat in range(4 * turn, 4 * turn + 4)]
        both = jnp.concatenate([regroup(*rows[:2]), regroup(*rows[2:])], axis=0)
        turned = dot(eye, both, NT)
        for step in range(4):
            row, column = step % 2 * waves, step // 2 * lanes
            lat = 4 * turn + step
            place = jnp.where(flip > 0, lat_rows - 1 - lat, lat)
            tile = turned[row : row + waves, column : column + lanes]
            spread[pl.ds(place, waves, stride=lat_rows + PAD), :] = tile
    for wave in range(waves):
        span = pl.ds(wave * (lat_rows + PAD), lat_rows)
        out_ref[owner_ref[wave]] = spread[span, :].astype(BF16)


def pack(x, owner, flip):
    lat_rows, level_count, field_count, lanes = x.shape
    waves = lanes // 2
    rows = lat_rows * level_count * field_count
    return pl.pallas_call(
        pack_kernel,
        out_shape=jax.ShapeDtypeStruct((waves, lat_rows, lanes), BF16),
        in_specs=[SMEM, SMEM, VMEM],
        out_specs=VMEM,
        scratch_shapes=[pltpu.VMEM((waves * (lat_rows + PAD), lanes), F32)],
        name="pack",
    )(owner, flip, x.reshape(rows, lanes))


def legendre_kernel(
    length_ref, weight_ref, x_ref, table_hbm, out_hbm, table, out_ref, folded, sems_in, sems_out
):
    blocks, slots, lat_rows, lanes = x_ref.shape
    half_blocks = blocks // 2

    def load(slot):
        return pltpu.make_async_copy(table_hbm.at[slot], table.at[slot], sems_in.at[slot])

    def store(slot):
        return pltpu.make_async_copy(out_ref.at[slot], out_hbm.at[:, slot], sems_out.at[slot])

    for slot in range(slots):
        load(slot).start()
    for slot in range(slots):
        for block in range(half_blocks):
            span = pl.ds(block * lat_rows, lat_rows)
            north = x_ref[block, slot].astype(F32)
            south = x_ref[blocks - 1 - block, slot].astype(F32)
            weight = weight_ref[span, :]
            folded[slot, 0, span, :] = (weight * (north + south)).astype(BF16)
            folded[slot, 1, span, :] = (weight * (north - south)).astype(BF16)
    for slot in range(slots):
        load(slot).wait()
        spectra = [dot(table[slot, parity], folded[slot, parity], NN) for parity in range(2)]
        turned = []
        for parity in range(2):
            degree = 2 * lax.broadcasted_iota(jnp.int32, spectra[parity].shape, 0) + parity
            live = jnp.where(degree < length_ref[slot], spectra[parity], 0.0)
            turned.append(live.T.astype(BF16))
        parts = [dot(turned[parity], table[slot, parity], NN) for parity in range(2)]
        upper = (parts[0] + parts[1]).T.astype(BF16)
        lower = (parts[0] - parts[1]).T.astype(BF16)
        for block in range(half_blocks):
            span = slice(block * lat_rows, (block + 1) * lat_rows)
            out_ref[slot, block] = upper[span]
            out_ref[slot, blocks - 1 - block] = lower[span]
        store(slot).start()
    for slot in range(slots):
        store(slot).wait()


def legendre_pair(x, table, weight, length):
    half_lats, lanes = weight.shape
    blocks, slots, lat_rows, lanes = x.shape
    return pl.pallas_call(
        legendre_kernel,
        out_shape=jax.ShapeDtypeStruct(x.shape, BF16),
        in_specs=[SMEM, VMEM, VMEM, HBM],
        out_specs=HBM,
        scratch_shapes=[
            pltpu.VMEM(table.shape, BF16),
            pltpu.VMEM((slots, blocks, lat_rows, lanes), BF16),
            pltpu.VMEM((slots, 2, half_lats, lanes), BF16),
            pltpu.SemaphoreType.DMA((slots,)),
            pltpu.SemaphoreType.DMA((slots,)),
        ],
        name="legendre",
        compiler_params=pltpu.CompilerParams(vmem_limit_bytes=50 * MIB),
    )(length, weight, x, table)


def totals_kernel(owner_ref, sum_ref, x_ref, out_ref, lines):
    waves, lat_rows, lanes = x_ref.shape
    weight = sum_ref[...]
    lines[...] = jnp.zeros_like(lines)
    for wave in range(waves):
        line = dot(weight, x_ref[owner_ref[wave]], NT)
        line = line[0:2] + line[2:4]
        lines[wave : wave + 1, :lat_rows] = line[0:1]
        lines[waves + wave : waves + wave + 1, :lat_rows] = line[1:2]
    out_ref[...] = lines[...].T[:lat_rows]


def totals(x, owner, weight):
    waves, lat_rows, lanes = x.shape
    return pl.pallas_call(
        totals_kernel,
        out_shape=jax.ShapeDtypeStruct((lat_rows, lanes), F32),
        in_specs=[SMEM, VMEM, VMEM],
        out_specs=VMEM,
        scratch_shapes=[pltpu.VMEM((lanes, lanes), F32)],
        name="totals",
        compiler_params=pltpu.CompilerParams(vmem_limit_bytes=6 * MIB),
    )(owner, weight, x)


def unpack_kernel(owner_ref, flip_ref, mix_ref, x_ref, out_hbm, geo_ref, out_ref, spread, sems):
    waves, lat_rows, lanes = x_ref.shape
    levels = geo_ref.shape[1]
    flip = flip_ref[0]
    parts = sems.shape[0]
    quads = lat_rows // 4 // parts
    rows = waves + 2 * levels

    def store(part):
        span = pl.ds(part * 4 * quads, 4 * quads)
        return pltpu.make_async_copy(out_ref.at[span], out_hbm.at[span], sems.at[part])

    for wave in range(waves):
        span = pl.ds(wave * (lat_rows + PAD), lat_rows)
        spread[span, :] = x_ref[owner_ref[wave]].astype(F32)
    for part in range(parts):
        for turn in range(part * quads, (part + 1) * quads):
            tiles = []
            for step in range(4):
                lat = 4 * turn + step
                place = jnp.where(flip > 0, lat_rows - 1 - lat, lat)
                tiles.append(spread[pl.ds(place, waves, stride=lat_rows + PAD), :].astype(BF16))
            both = jnp.concatenate([regroup(*tiles[:2]), regroup(*tiles[2:])], axis=0)
            turned = dot(mix_ref[...], both, NT)
            for step in range(4):
                lat = 4 * turn + step
                side = turned[:, step // 2 * lanes : (step // 2 + 1) * lanes]
                side = side[step % 2 * rows : (step % 2 + 1) * rows]
                out_ref[lat] = side[:waves].astype(BF16)
                geo_ref[lat] = side[waves : waves + levels] + side[waves + levels :]
        store(part).start()
    for part in range(parts):
        store(part).wait()


def unpack(x, owner, flip, mix, levels):
    waves, lat_rows, lanes = x.shape
    return pl.pallas_call(
        unpack_kernel,
        out_shape=(
            jax.ShapeDtypeStruct((lat_rows, waves, lanes), BF16),
            jax.ShapeDtypeStruct((lat_rows, levels, lanes), F32),
        ),
        in_specs=[SMEM, SMEM, VMEM, VMEM],
        out_specs=(HBM, VMEM),
        scratch_shapes=[
            pltpu.VMEM((lat_rows, waves, lanes), BF16),
            pltpu.VMEM((waves * (lat_rows + PAD), lanes), F32),
            pltpu.SemaphoreType.DMA((5,)),
        ],
        name="unpack",
        compiler_params=pltpu.CompilerParams(vmem_limit_bytes=12 * MIB),
    )(owner, flip, mix, x)


def finish_kernel(flip_ref, inside_ref, own_ref, *refs):
    *later_refs, out_ref, below = refs
    lat_rows = out_ref.shape[0]
    flip = flip_ref[0]
    state = jnp.where(flip_ref[1] % 2 == 0, own_ref[...], 0.0)
    for step, ref in enumerate(later_refs):
        ahead = flip_ref[1] // 2 + step + 1 <= len(later_refs)
        state = state + jnp.where(ahead, ref[...], 0.0)
    below[...] = state
    for lat in range(lat_rows):
        place = jnp.where(flip > 0, lat_rows - 1 - lat, lat)
        out_ref[lat] = (inside_ref[lat] + below[pl.ds(place, 1), :]).astype(BF16)


def finish(flags, inside, other, later):
    lat_rows, levels, lanes = inside.shape
    return pl.pallas_call(
        finish_kernel,
        out_shape=jax.ShapeDtypeStruct(inside.shape, BF16),
        in_specs=[SMEM] + [VMEM] * (2 + len(later)),
        out_specs=VMEM,
        scratch_shapes=[pltpu.VMEM((lat_rows, lanes), F32)],
        name="finish",
        compiler_params=pltpu.CompilerParams(vmem_limit_bytes=6 * MIB),
    )(flags, inside, other, *later)


def two_terms(weight):
    high = lax.reduce_precision(weight, 8, 7)
    return high.astype(BF16), (weight - high).astype(BF16)


def level_sums(layer_depth, field_count):
    levels = layer_depth.shape[0]
    columns = levels * field_count
    to = jnp.arange(levels)[:, None]
    column = jnp.arange(columns)[None, :]
    level = column // field_count
    depth = jnp.repeat(layer_depth, field_count)[None, :]
    depth = jnp.where(column % field_count == 0, depth, 0.0)
    share = jnp.where(to == level, 0.5, jnp.where(to < level, 1.0, 0.0))

    eye = jnp.eye(columns, dtype=BF16)
    inside = jnp.concatenate((eye,) + two_terms(share * depth), axis=0)
    blank = jnp.zeros_like(inside)
    mix = jnp.concatenate(
        [jnp.concatenate(pair, axis=1) for pair in ((inside, blank), (blank, inside))], axis=0
    )
    high, low = two_terms(depth)
    blank = jnp.zeros_like(high)
    pieces = ((high, blank), (blank, high), (low, blank), (blank, low))
    every = [jnp.concatenate(piece, axis=1) for piece in pieces]
    every = jnp.concatenate(every + [jnp.zeros((4, 2 * columns), BF16)], axis=0)
    return mix, every


def sums_of_later(total):
    count = lax.axis_size("lev")
    other = lax.ppermute(total, "lev", [(i, i ^ 1) for i in range(count)])
    both = total + other
    later = [
        lax.ppermute(both, "lev", [(i, (i - step) % count) for i in range(count)])
        for step in range(2, count, 2)
    ]
    return other, later


def on_device(fourier, owner, legendre, quad_weights, layer_depth):
    lat_rows, level_count, field_count, doubled = fourier.shape
    waves = doubled // 2
    slots = legendre.shape[0]
    degrees = 2 * legendre.shape[2]
    blocks = waves // slots
    place = lax.axis_index("wave")
    flip = (place >= blocks // 2).astype(jnp.int32).reshape(1)
    mine = place * slots + jnp.arange(slots, dtype=jnp.int32)
    wave_ids = jnp.arange(waves, dtype=jnp.int32)
    my_waves = jnp.sum(jnp.where(owner[None, :] == mine[:, None], wave_ids[None, :], 0), axis=1)
    lengths = degrees - my_waves * degrees // waves
    weight = jnp.broadcast_to(quad_weights[:, None], (quad_weights.shape[0], doubled))
    mix, every = level_sums(layer_depth, field_count)
    lev = lax.axis_index("lev").astype(jnp.int32).reshape(1)

    outgoing = pack(fourier, owner, flip)
    arrived = lax.all_to_all(outgoing, "wave", split_axis=0, concat_axis=0, tiled=True)
    arrived = arrived.reshape(blocks, slots, lat_rows, doubled)
    results = legendre_pair(arrived, legendre, weight, lengths)
    results = results.reshape(waves, lat_rows, doubled)
    returned = lax.all_to_all(results, "wave", split_axis=0, concat_axis=0, tiled=True)
    other, later = sums_of_later(totals(returned, owner, every))
    fields, inside = unpack(returned, owner, flip, mix, level_count)
    fields_out = fields.reshape(fourier.shape)
    geopotential = finish(jnp.concatenate([flip, lev]), inside, other, later)
    return (fields_out, geopotential)


def solution(mesh):
    return jax.shard_map(
        on_device,
        mesh=mesh,
        in_specs=(P("wave", "lev", None, None), P(), P("wave", None, None, None), P(), P("lev")),
        out_specs=(P("wave", "lev", None, None), P("wave", "lev", None)),
        check_vma=False,
    )
```

time: 127 us -> 108 us (0.85)
  blocking collectives: 13.4 us -> 0 us
  Pallas kernels: 23.7 us -> 15.7 us
  starting transfers between devices: 18.2 us -> 22.7 us
  waiting for transfers between devices: 64.3 us -> 67.5 us
  other arithmetic: 2.81 us -> 0.41 us
  local copies, waits for them, and re-layouts: 2.76 us -> 0.6 us
    all_gather x1 -> x0, blocking collectives: 13.4 us -> none  [on_device(): gathered = lax.all_gather(total, 'lev')]
    ppermute x0 -> x4, starting transfers between devices: none -> 4.53 us  [the longest x3 4.44 us: sums_of_later(): lax.ppermute(both, 'lev', [(i, (i - step) % count) for i in range(count)])]
    pallas_call x1, Pallas kernels: 6.79 us -> 2.74 us  [unpack(): pl.pallas_call(unpack_kernel, out_shape=(jax.ShapeDtypeStruct((lat_rows,...]
    pallas_call x1, Pallas kernels: 10.7 us -> 6.86 us  [legendre_pair(): pl.pallas_call(legendre_kernel, out_shape=jax.ShapeDtypeStruct(x.shape, B...]
    pallas_call x1, Pallas kernels: 6.29 us -> 3.29 us  [pack(): pl.pallas_call(pack_kernel, out_shape=jax.ShapeDtypeStruct((waves, lat_ro...]
    pallas_call x0 -> x2, Pallas kernels: none -> 2.79 us  [the longest x1 1.42 us: totals(): pl.pallas_call(totals_kernel, out_shape=jax.ShapeDtypeStruct((lat_rows, l...]
    ppermute x0 -> x4, waiting for transfers between devices: none -> 2.61 us  [the longest x3 1.49 us: sums_of_later(): lax.ppermute(both, 'lev', [(i, (i - step) % count) for i in range(count)])]
    convert_element_type x2 -> x4, other arithmetic: 1.97 us -> 0.03 us  [the longest x3 0.02 us: two_terms(): return (high.astype(BF16), (weight - high).astype(BF16))]
  transfers between devices with their start and end apart: 2 -> 6, of which waited for: 2 -> 5; matrix products, arithmetic and copies ran while one was open for 1% -> 1% of each run, Pallas kernels for 0% -> 3%
where the time goes in v2:
time: 108 us
  waiting for transfers between devices  67.5 us (62%)
  starting transfers between devices  22.7 us (21%)
  Pallas kernels  15.7 us (15%)
    all_to_all x1, waiting for transfers between devices, on_device(): lax.all_to_all(outgoing, 'wave', split_axis=0, concat_axis=0, tiled=True)  32.7 us
    all_to_all x1, waiting for transfers between devices, on_device(): lax.all_to_all(results, 'wave', split_axis=0, concat_axis=0, tiled=True)  32.2 us
    all_to_all x1, starting transfers between devices, on_device(): lax.all_to_all(outgoing, 'wave', split_axis=0, concat_axis=0, tiled=True)  11.8 us
    pallas_call x1, Pallas kernels, legendre_pair(): pl.pallas_call(legendre_kernel, out_shape=jax.ShapeDtypeStruct(x.shape, B...  6.86 us
    all_to_all x1, starting transfers between devices, on_device(): lax.all_to_all(results, 'wave', split_axis=0, concat_axis=0, tiled=True)  6.35 us
    ppermute x3, starting transfers between devices, sums_of_later(): lax.ppermute(both, 'lev', [(i, (i - step) % count) for i in range(count)])  4.44 us
    pallas_call x1, Pallas kernels, pack(): pl.pallas_call(pack_kernel, out_shape=jax.ShapeDtypeStruct((waves, lat_ro...  3.29 us
    pallas_call x1, Pallas kernels, unpack(): pl.pallas_call(unpack_kernel, out_shape=(jax.ShapeDtypeStruct((lat_rows,...  2.74 us
  transfers between devices with their start and end apart: 6, of which 5 were waited for; matrix products, arithmetic and copies ran while one was open for 1% of the time, Pallas kernels for 3%

profile of v2, /device:TPU:8, one launch (start us, length us, event | category | flops | bytes accessed | tf_op | source)
XLA Modules:
  0.0 107.7 jit_solution(13762269625691112786)
XLA Ops:
  0.6 3.3 %pack.1 = bf16[64,80,128]{2,1,0:T(8,128)(2,1)} custom-call(s32[64]{0:T(128)} %owner_ref.5, s32[1]{0:T(128)} %bitcast.flip_ref, bf16[5120,128]{1,0:T(8,128)(2,1)} %bitcast.7), custom_call_target="tpu_custom_call" | custom-call | tf_op jit(solution)/shard_map/pack/pallas_call | solution.py:64
  3.9 11.8 %all-to-all-start = ((bf16[64,80,128]{2,1,0:T(8,128)(2,1)}), bf16[64,80,128]{2,1,0:T(8,128)(2,1)S(1)}, u32[]{:S(2)}, u32[]{:S(2)}) async-start(bf16[64,80,128]{2,1,0:T(8,128)(2,1)} %pack.1), calls=%async_computation | async-start | bytes 2621440 | tf_op jit(solution)/shard_map/all_to_all | solution.py:300
  15.8 0.2 fusion.5
  16.0 32.7 %all-to-all-done = bf16[64,80,128]{2,1,0:T(8,128)(2,1)S(1)} async-done(((bf16[64,80,128]{2,1,0:T(8,128)(2,1)}), bf16[64,80,128]{2,1,0:T(8,128)(2,1)S(1)}, u32[]{:S(2)}, u32[]{:S(2)}) %all-to-all-start) | async-done | bytes 1310752 | tf_op jit(solution)/shard_map/all_to_all | solution.py:300
  48.7 0.2 broadcast_in_dim.56.weight_ref
  48.9 6.9 %legendre.1 = bf16[32,2,80,128]{3,2,1,0:T(8,128)(2,1)} custom-call(s32[2]{0:T(128)S(1)} %fusion.7.length_ref, f32[1280,128]{1,0:T(8,128)S(1)} %broadcast_in_dim.56.weight_ref, bf16[32,2,80,128]{3,2,1,0:T(8,128)(2,1)S(1)} %bitcast.6, bf16[2,2,640,1280]{3,2,1,0:T(8,128)(2,1)} %table_hbm.1), custom_call_target="tpu_custom_call" | custom-call | tf_op jit(solution)/shard_map/legendre/pallas_call | solution.py:119
  55.8 6.4 %all-to-all-start.1 = ((bf16[64,80,128]{2,1,0:T(8,128)(2,1)}), bf16[64,80,128]{2,1,0:T(8,128)(2,1)S(1)}, u32[]{:S(2)}, u32[]{:S(2)}) async-start(bf16[64,80,128]{2,1,0:T(8,128)(2,1)} %bitcast.3), calls=%async_computation.1 | async-start | bytes 2621440 | tf_op jit(solution)/shard_map/all_to_all | solution.py:304
  62.2 0.1 broadcast_in_dim.52
  62.2 0.1 broadcast_in_dim_reshape.5
  62.3 0.1 broadcast_in_dim_reshape.6
  62.4 0.1 fusion.8
  62.6 32.2 %all-to-all-done.1.x_ref = bf16[64,80,128]{2,1,0:T(8,128)(2,1)S(1)} async-done(((bf16[64,80,128]{2,1,0:T(8,128)(2,1)}), bf16[64,80,128]{2,1,0:T(8,128)(2,1)S(1)}, u32[]{:S(2)}, u32[]{:S(2)}) %all-to-all-start.1) | async-done | bytes 1310752 | tf_op jit(solution)/shard_map/all_to_all | solution.py:304
  94.8 1.4 %totals.1 = f32[80,128]{1,0:T(8,128)S(1)} custom-call(s32[64]{0:T(128)S(1)} %copy-done, bf16[8,128]{1,0:T(8,128)(2,1)S(1)} %concatenate.39.sum_ref, bf16[64,80,128]{2,1,0:T(8,128)(2,1)S(1)} %all-to-all-done.1.x_ref), custom_call_target="tpu_custom_call" | custom-call | tf_op jit(solution)/shard_map/totals/pallas_call | solution.py:150
  96.2 0.1 collective-permute-start
  96.3 0.1 fusion.2.mix_ref
  96.4 1.1 %collective-permute-done.own_ref = f32[80,128]{1,0:T(8,128)S(1)} collective-permute-done((f32[80,128]{1,0:T(8,128)S(1)}, f32[80,128]{1,0:T(8,128)S(1)}, u32[]{:S(2)}, u32[]{:S(2)}) %collective-permute-start) | collective-permute-done | bytes 40992 | tf_op jit(solution)/shard_map/ppermute | solution.py:274
  97.5 2.8 %collective-permute-start.1 = (f32[80,128]{1,0:T(8,128)S(1)}, f32[80,128]{1,0:T(8,128)S(1)}, u32[]{:S(2)}, u32[]{:S(2)}) collective-permute-start(f32[80,128]{1,0:T(8,128)S(1)} %add.59), channel_id=1, source_target_pairs={{0,6},{1,7},{2,0},{3,1},{4,2},{5,3},{6,4},{7,5},{8,14},{9,15},{10,... | collective-permute-start | bytes 122888 | tf_op jit(solution)/shard_map/ppermute | solution.py:277
  100.3 0.8 collective-permute-start.2
  101.1 0.9 collective-permute-start.3
  102.0 0.1 pad_add_fusion.flip_ref
  102.0 2.7 %unpack.1 = (bf16[80,64,128]{2,1,0:T(8,128)(2,1)}, f32[80,16,128]{2,1,0:T(8,128)S(1)}) custom-call(s32[64]{0:T(128)S(1)} %copy-done, s32[1]{0:T(128)} %bitcast.flip_ref, bf16[192,128]{1,0:T(8,128)(2,1)S(1)} %fusion.2.mix_ref, bf16[64,80,128]{2,1,0:T(8,128)(2,1)S(1)} %all-to-all-done.1.x_ref), custom_call_target="tpu_custom_call" | custom-call | tf_op jit(solution)/shard_map/unpack/pallas_call | solution.py:198
  104.8 1.0 collective-permute-done.2.refs_1_
  105.8 0.5 collective-permute-done.3.refs_2_
  106.3 1.4 %finish.1 = bf16[80,16,128]{2,1,0:T(8,128)(2,1)} custom-call(s32[2]{0:T(128)S(1)} %pad_add_fusion.flip_ref, f32[80,16,128]{2,1,0:T(8,128)S(1)} %get-tuple-element.5.inside_ref, f32[80,128]{1,0:T(8,128)S(1)} %collective-permute-done.own_ref, f32[80,128]{1,0:T(8,128)S(1)} %collective-permute-done.1.refs_0_, f32[80,128]{1,0:T(8,128)S(1)} %collective-permute-done.2.refs_1_, ...), custom_call_target="tpu_custom_call" | custom-call | tf_op jit(solution)/shard_map/finish/pallas_call | solution.py:232
  (19 shorter events, 0.1 us)
Async XLA Ops:
  3.9 11.9 %copy-start = (s32[64]{0:T(128)S(1)}, s32[64]{0:T(128)}, u32[]{:S(2)}) copy-start(s32[64]{0:T(128)} %owner_ref.5) | copy-start | bytes 772
  3.9 44.8 %copy-start.1 = (f32[1280]{0:T(1024)S(1)}, f32[1280]{0:T(1024)}, u32[]{:S(2)}) copy-start(f32[1280]{0:T(1024)} %param.8) | copy-start | bytes 15364
  3.9 44.7 %all-to-all-start = ((bf16[64,80,128]{2,1,0:T(8,128)(2,1)}), bf16[64,80,128]{2,1,0:T(8,128)(2,1)S(1)}, u32[]{:S(2)}, u32[]{:S(2)}) async-start(bf16[64,80,128]{2,1,0:T(8,128)(2,1)} %pack.1), calls=%async_computation | async-start | bytes 2621440 | tf_op jit(solution)/shard_map/all_to_all | solution.py:300
  55.8 6.4 %copy-start.2 = (f32[16]{0:T(128)S(1)}, f32[16]{0:T(128)}, u32[]{:S(2)}) copy-start(f32[16]{0:T(128)} %param.9) | copy-start | bytes 196
  55.8 39.0 %all-to-all-start.1 = ((bf16[64,80,128]{2,1,0:T(8,128)(2,1)}), bf16[64,80,128]{2,1,0:T(8,128)(2,1)S(1)}, u32[]{:S(2)}, u32[]{:S(2)}) async-start(bf16[64,80,128]{2,1,0:T(8,128)(2,1)} %bitcast.3), calls=%async_computation.1 | async-start | bytes 2621440 | tf_op jit(solution)/shard_map/all_to_all | solution.py:304
  96.2 1.3 %collective-permute-start = (f32[80,128]{1,0:T(8,128)S(1)}, f32[80,128]{1,0:T(8,128)S(1)}, u32[]{:S(2)}, u32[]{:S(2)}) collective-permute-start(f32[80,128]{1,0:T(8,128)S(1)} %totals.1), channel_id=1, source_target_pairs={{0,1},{1,0},{2,3},{3,2},{4,5},{5,4},{6,7},{7,6},{8,9},{9,8},{10,11... | collective-permute-start | bytes 122888 | tf_op jit(solution)/shard_map/ppermute | solution.py:274
  97.5 7.3 %collective-permute-start.1 = (f32[80,128]{1,0:T(8,128)S(1)}, f32[80,128]{1,0:T(8,128)S(1)}, u32[]{:S(2)}, u32[]{:S(2)}) collective-permute-start(f32[80,128]{1,0:T(8,128)S(1)} %add.59), channel_id=1, source_target_pairs={{0,6},{1,7},{2,0},{3,1},{4,2},{5,3},{6,4},{7,5},{8,14},{9,15},{10,... | collective-permute-start | bytes 122888 | tf_op jit(solution)/shard_map/ppermute | solution.py:277
  100.3 5.5 %collective-permute-start.2 = (f32[80,128]{1,0:T(8,128)S(1)}, f32[80,128]{1,0:T(8,128)S(1)}, u32[]{:S(2)}, u32[]{:S(2)}) collective-permute-start(f32[80,128]{1,0:T(8,128)S(1)} %add.59), channel_id=1, source_target_pairs={{0,4},{1,5},{2,6},{3,7},{4,0},{5,1},{6,2},{7,3},{8,12},{9,13},{10,... | collective-permute-start | bytes 122888 | tf_op jit(solution)/shard_map/ppermute | solution.py:277
  101.1 5.2 %collective-permute-start.3 = (f32[80,128]{1,0:T(8,128)S(1)}, f32[80,128]{1,0:T(8,128)S(1)}, u32[]{:S(2)}, u32[]{:S(2)}) collective-permute-start(f32[80,128]{1,0:T(8,128)S(1)} %add.59), channel_id=1, source_target_pairs={{0,2},{1,3},{2,4},{3,5},{4,6},{5,7},{6,0},{7,1},{8,10},{9,11},{10,... | collective-permute-start | bytes 122888 | tf_op jit(solution)/shard_map/ppermute | solution.py:277

commit v3 on v2

--- a/solution.py
+++ b/solution.py
@@ -21,6 +21,10 @@
     return lax.dot_general(a, b, dims, preferred_element_type=F32)
 
 
+def northern():
+    return lax.axis_index("wave") < lax.axis_size("wave") // 2
+
+
 def identity(size):
     rows = lax.broadcasted_iota(jnp.int32, (size, size), 0)
     cols = lax.broadcasted_iota(jnp.int32, (size, size), 1)
@@ -38,41 +42,78 @@
     )
 
 
-def pack_kernel(owner_ref, flip_ref, x_ref, out_ref, spread):
+def pack_kernel(
+    owner_hbm, x_hbm, out_hbm, owner_ref, wave_of, x_ref, out_ref, spread, sems, sems_out
+):
     waves, lat_rows, lanes = out_ref.shape
+    first = lat_rows // 5 * waves
+    spans = (pl.ds(0, first), pl.ds(first, lat_rows * waves - first))
+    loads = [
+        pltpu.make_async_copy(x_hbm.at[span], x_ref.at[span], sems.at[part])
+        for part, span in enumerate(spans)
+    ]
+    loads.append(pltpu.make_async_copy(owner_hbm, owner_ref, sems.at[2]))
+    for load in loads:
+        load.start()
     eye = identity(lanes)
-    flip = flip_ref[0]
+    north = northern()
     for turn in range(lat_rows // 4):
+        if turn == 0:
+            loads[0].wait()
+        if 4 * turn * waves == first:
+            loads[1].wait()
+            loads[2].wait()
+            for wave in range(waves):
+                wave_of[owner_ref[wave]] = wave
         rows = [x_ref[lat * waves : (lat + 1) * waves, :] for lat in range(4 * turn, 4 * turn + 4)]
         both = jnp.concatenate([regroup(*rows[:2]), regroup(*rows[2:])], axis=0)
         turned = dot(eye, both, NT)
         for step in range(4):
             row, column = step % 2 * waves, step // 2 * lanes
             lat = 4 * turn + step
-            place = jnp.where(flip > 0, lat_rows - 1 - lat, lat)
+            place = jnp.where(north, lat, lat_rows - 1 - lat)
             tile = turned[row : row + waves, column : column + lanes]
             spread[pl.ds(place, waves, stride=lat_rows + PAD), :] = tile
-    for wave in range(waves):
-        span = pl.ds(wave * (lat_rows + PAD), lat_rows)
-        out_ref[owner_ref[wave]] = spread[span, :].astype(BF16)
-
-
-def pack(x, owner, flip):
+    parts = sems_out.shape[0]
+    size = waves // parts
+    stores = []
+    for part in range(parts):
+        for slot in range(part * size, (part + 1) * size):
+            start = pl.multiple_of(wave_of[slot] * (lat_rows + PAD), 8)
+            out_ref[slot] = spread[pl.ds(start, lat_rows), :].astype(BF16)
+        span = pl.ds(part * size, size)
+        stores.append(
+            pltpu.make_async_copy(out_ref.at[span], out_hbm.at[span], sems_out.at[part])
+        )
+        stores[-1].start()
+    for store in stores:
+        store.wait()
+
+
+def pack(x, owner):
     lat_rows, level_count, field_count, lanes = x.shape
     waves = lanes // 2
     rows = lat_rows * level_count * field_count
     return pl.pallas_call(
         pack_kernel,
         out_shape=jax.ShapeDtypeStruct((waves, lat_rows, lanes), BF16),
-        in_specs=[SMEM, SMEM, VMEM],
-        out_specs=VMEM,
-        scratch_shapes=[pltpu.VMEM((waves * (lat_rows + PAD), lanes), F32)],
+        in_specs=[HBM, HBM],
+        out_specs=HBM,
+        scratch_shapes=[
+            pltpu.SMEM((waves,), jnp.int32),
+            pltpu.SMEM((waves,), jnp.int32),
+            pltpu.VMEM((rows, lanes), BF16),
+            pltpu.VMEM((waves, lat_rows, lanes), BF16),
+            pltpu.VMEM(((waves + 1) * (lat_rows + PAD), lanes), F32),
+            pltpu.SemaphoreType.DMA((3,)),
+            pltpu.SemaphoreType.DMA((4,)),
+        ],
         name="pack",
-    )(owner, flip, x.reshape(rows, lanes))
+    )(owner, x.reshape(rows, lanes))
 
 
 def legendre_kernel(
-    length_ref, weight_ref, x_ref, table_hbm, out_hbm, table, out_ref, folded, sems_in, sems_out
+    weight_ref, x_ref, table_hbm, out_hbm, table, out_ref, folded, sems_in, sems_out
 ):
     blocks, slots, lat_rows, lanes = x_ref.shape
     half_blocks = blocks // 2
@@ -93,33 +134,47 @@
             weight = weight_ref[span, :]
             folded[slot, 0, span, :] = (weight * (north + south)).astype(BF16)
             folded[slot, 1, span, :] = (weight * (north - south)).astype(BF16)
-    for slot in range(slots):
-        load(slot).wait()
+    def forward(slot):
         spectra = [dot(table[slot, parity], folded[slot, parity], NN) for parity in range(2)]
+        row = half_blocks * lat_rows + slot
+        length = weight_ref[row : row + 1, :]
         turned = []
         for parity in range(2):
             degree = 2 * lax.broadcasted_iota(jnp.int32, spectra[parity].shape, 0) + parity
-            live = jnp.where(degree < length_ref[slot], spectra[parity], 0.0)
+            live = jnp.where(degree.astype(F32) < length, spectra[parity], 0.0)
             turned.append(live.T.astype(BF16))
-        parts = [dot(turned[parity], table[slot, parity], NN) for parity in range(2)]
+        return turned
+
+    def inverse(slot, turned):
+        return [dot(turned[parity], table[slot, parity], NN) for parity in range(2)]
+
+    def finish(slot, parts):
         upper = (parts[0] + parts[1]).T.astype(BF16)
         lower = (parts[0] - parts[1]).T.astype(BF16)
         for block in range(half_blocks):
             span = slice(block * lat_rows, (block + 1) * lat_rows)
             out_ref[slot, block] = upper[span]
             out_ref[slot, blocks - 1 - block] = lower[span]
-        store(slot).start()
-    for slot in range(slots):
-        store(slot).wait()
-
-
-def legendre_pair(x, table, weight, length):
-    half_lats, lanes = weight.shape
+
+    load(0).wait()
+    turned = forward(0)
+    load(1).wait()
+    other = forward(1)
+    finish(0, inverse(0, turned))
+    store(0).start()
+    finish(1, inverse(1, other))
+    store(1).start()
+    store(0).wait()
+    store(1).wait()
+
+
+def legendre_pair(x, table, weight):
     blocks, slots, lat_rows, lanes = x.shape
+    half_lats = blocks // 2 * lat_rows
     return pl.pallas_call(
         legendre_kernel,
         out_shape=jax.ShapeDtypeStruct(x.shape, BF16),
-        in_specs=[SMEM, VMEM, VMEM, HBM],
+        in_specs=[VMEM, VMEM, HBM],
         out_specs=HBM,
         scratch_shapes=[
             pltpu.VMEM(table.shape, BF16),
@@ -130,7 +185,7 @@
         ],
         name="legendre",
         compiler_params=pltpu.CompilerParams(vmem_limit_bytes=50 * MIB),
-    )(length, weight, x, table)
+    )(weight, x, table)
 
 
 def totals_kernel(owner_ref, sum_ref, x_ref, out_ref, lines):
@@ -158,10 +213,10 @@
     )(owner, weight, x)
 
 
-def unpack_kernel(owner_ref, flip_ref, mix_ref, x_ref, out_hbm, geo_ref, out_ref, spread, sems):
+def unpack_kernel(owner_ref, mix_ref, x_ref, out_hbm, geo_ref, out_ref, spread, sems):
     waves, lat_rows, lanes = x_ref.shape
     levels = geo_ref.shape[1]
-    flip = flip_ref[0]
+    north = northern()
     parts = sems.shape[0]
     quads = lat_rows // 4 // parts
     rows = waves + 2 * levels
@@ -178,7 +233,7 @@
             tiles = []
             for step in range(4):
                 lat = 4 * turn + step
-                place = jnp.where(flip > 0, lat_rows - 1 - lat, lat)
+                place = jnp.where(north, lat, lat_rows - 1 - lat)
                 tiles.append(spread[pl.ds(place, waves, stride=lat_rows + PAD), :].astype(BF16))
             both = jnp.concatenate([regroup(*tiles[:2]), regroup(*tiles[2:])], axis=0)
             turned = dot(mix_ref[...], both, NT)
@@ -193,7 +248,7 @@
         store(part).wait()
 
 
-def unpack(x, owner, flip, mix, levels):
+def unpack(x, owner, mix, levels):
     waves, lat_rows, lanes = x.shape
     return pl.pallas_call(
         unpack_kernel,
@@ -201,43 +256,44 @@
             jax.ShapeDtypeStruct((lat_rows, waves, lanes), BF16),
             jax.ShapeDtypeStruct((lat_rows, levels, lanes), F32),
         ),
-        in_specs=[SMEM, SMEM, VMEM, VMEM],
+        in_specs=[SMEM, VMEM, VMEM],
         out_specs=(HBM, VMEM),
         scratch_shapes=[
             pltpu.VMEM((lat_rows, waves, lanes), BF16),
-            pltpu.VMEM((waves * (lat_rows + PAD), lanes), F32),
+            pltpu.VMEM(((waves + 1) * (lat_rows + PAD), lanes), F32),
             pltpu.SemaphoreType.DMA((5,)),
         ],
         name="unpack",
         compiler_params=pltpu.CompilerParams(vmem_limit_bytes=12 * MIB),
-    )(owner, flip, mix, x)
-
-
-def finish_kernel(flip_ref, inside_ref, own_ref, *refs):
+    )(owner, mix, x)
+
+
+def finish_kernel(inside_ref, own_ref, *refs):
     *later_refs, out_ref, below = refs
     lat_rows = out_ref.shape[0]
-    flip = flip_ref[0]
-    state = jnp.where(flip_ref[1] % 2 == 0, own_ref[...], 0.0)
+    north = northern()
+    lev = lax.axis_index("lev")
+    state = jnp.where(lev % 2 == 0, own_ref[...], 0.0)
     for step, ref in enumerate(later_refs):
-        ahead = flip_ref[1] // 2 + step + 1 <= len(later_refs)
+        ahead = lev // 2 + step + 1 <= len(later_refs)
         state = state + jnp.where(ahead, ref[...], 0.0)
     below[...] = state
     for lat in range(lat_rows):
-        place = jnp.where(flip > 0, lat_rows - 1 - lat, lat)
+        place = jnp.where(north, lat, lat_rows - 1 - lat)
         out_ref[lat] = (inside_ref[lat] + below[pl.ds(place, 1), :]).astype(BF16)
 
 
-def finish(flags, inside, other, later):
+def finish(inside, other, later):
     lat_rows, levels, lanes = inside.shape
     return pl.pallas_call(
         finish_kernel,
         out_shape=jax.ShapeDtypeStruct(inside.shape, BF16),
-        in_specs=[SMEM] + [VMEM] * (2 + len(later)),
+        in_specs=[VMEM] * (2 + len(later)),
         out_specs=VMEM,
         scratch_shapes=[pltpu.VMEM((lat_rows, lanes), F32)],
         name="finish",
         compiler_params=pltpu.CompilerParams(vmem_limit_bytes=6 * MIB),
-    )(flags, inside, other, *later)
+    )(inside, other, *later)
 
 
 def two_terms(weight):
@@ -287,25 +343,24 @@
     degrees = 2 * legendre.shape[2]
     blocks = waves // slots
     place = lax.axis_index("wave")
-    flip = (place >= blocks // 2).astype(jnp.int32).reshape(1)
     mine = place * slots + jnp.arange(slots, dtype=jnp.int32)
     wave_ids = jnp.arange(waves, dtype=jnp.int32)
     my_waves = jnp.sum(jnp.where(owner[None, :] == mine[:, None], wave_ids[None, :], 0), axis=1)
     lengths = degrees - my_waves * degrees // waves
-    weight = jnp.broadcast_to(quad_weights[:, None], (quad_weights.shape[0], doubled))
+    lines = jnp.concatenate([quad_weights, lengths.astype(F32), jnp.zeros((8 - slots,), F32)])
+    weight = jnp.broadcast_to(lines[:, None], (lines.shape[0], doubled))
     mix, every = level_sums(layer_depth, field_count)
-    lev = lax.axis_index("lev").astype(jnp.int32).reshape(1)
-
-    outgoing = pack(fourier, owner, flip)
+
+    outgoing = pack(fourier, owner)
     arrived = lax.all_to_all(outgoing, "wave", split_axis=0, concat_axis=0, tiled=True)
     arrived = arrived.reshape(blocks, slots, lat_rows, doubled)
-    results = legendre_pair(arrived, legendre, weight, lengths)
+    results = legendre_pair(arrived, legendre, weight)
     results = results.reshape(waves, lat_rows, doubled)
     returned = lax.all_to_all(results, "wave", split_axis=0, concat_axis=0, tiled=True)
     other, later = sums_of_later(totals(returned, owner, every))
-    fields, inside = unpack(returned, owner, flip, mix, level_count)
+    fields, inside = unpack(returned, owner, mix, level_count)
     fields_out = fields.reshape(fourier.shape)
-    geopotential = finish(jnp.concatenate([flip, lev]), inside, other, later)
+    geopotential = finish(inside, other, later)
     return (fields_out, geopotential)
 
 

time: 108 us -> 106 us (0.981)
  Pallas kernels: 15.7 us -> 14.1 us
where the time goes in v3:
time: 106 us
  waiting for transfers between devices  67.5 us (64%)
  starting transfers between devices  22.6 us (21%)
  Pallas kernels  14.1 us (13%)
    all_to_all x1, waiting for transfers between devices, on_device(): lax.all_to_all(outgoing, 'wave', split_axis=0, concat_axis=0, tiled=True)  32.6 us
    all_to_all x1, waiting for transfers between devices, on_device(): lax.all_to_all(results, 'wave', split_axis=0, concat_axis=0, tiled=True)  32.2 us
    all_to_all x1, starting transfers between devices, on_device(): lax.all_to_all(outgoing, 'wave', split_axis=0, concat_axis=0, tiled=True)  11.7 us
    all_to_all x1, starting transfers between devices, on_device(): lax.all_to_all(results, 'wave', split_axis=0, concat_axis=0, tiled=True)  6.35 us
    pallas_call x1, Pallas kernels, legendre_pair(): pl.pallas_call(legendre_kernel, out_shape=jax.ShapeDtypeStruct(x.shape, B...  6.07 us
    ppermute x3, starting transfers between devices, sums_of_later(): lax.ppermute(both, 'lev', [(i, (i - step) % count) for i in range(count)])  4.45 us
    pallas_call x1, Pallas kernels, pack(): pl.pallas_call(pack_kernel, out_shape=jax.ShapeDtypeStruct((waves, lat_ro...  3.1 us
    pallas_call x1, Pallas kernels, unpack(): pl.pallas_call(unpack_kernel, out_shape=(jax.ShapeDtypeStruct((lat_rows,...  2.71 us
  transfers between devices with their start and end apart: 6, of which 5 were waited for; matrix products, arithmetic and copies ran while one was open for 1% of the time, Pallas kernels for 3%

profile of v3, /device:TPU:8, one launch (start us, length us, event | category | flops | bytes accessed | tf_op | source)
XLA Modules:
  0.0 106.0 jit_solution(958783688803664949)
XLA Ops:
  0.6 3.1 %pack.1 = bf16[64,80,128]{2,1,0:T(8,128)(2,1)} custom-call(s32[64]{0:T(128)} %owner_ref.3, bf16[5120,128]{1,0:T(8,128)(2,1)} %bitcast.5), custom_call_target="tpu_custom_call" | custom-call | tf_op jit(solution)/shard_map/pack/pallas_call | solution.py:97
  3.8 11.7 %all-to-all-start = ((bf16[64,80,128]{2,1,0:T(8,128)(2,1)}), bf16[64,80,128]{2,1,0:T(8,128)(2,1)S(1)}, u32[]{:S(2)}, u32[]{:S(2)}) async-start(bf16[64,80,128]{2,1,0:T(8,128)(2,1)} %pack.1), calls=%async_computation | async-start | bytes 2621440 | tf_op jit(solution)/shard_map/all_to_all | solution.py:355
  15.5 0.2 fusion.5
  15.7 0.1 concatenate.34
  15.8 32.6 %all-to-all-done = bf16[64,80,128]{2,1,0:T(8,128)(2,1)S(1)} async-done(((bf16[64,80,128]{2,1,0:T(8,128)(2,1)}), bf16[64,80,128]{2,1,0:T(8,128)(2,1)S(1)}, u32[]{:S(2)}, u32[]{:S(2)}) %all-to-all-start) | async-done | bytes 1310752 | tf_op jit(solution)/shard_map/all_to_all | solution.py:355
  48.4 0.2 broadcast_in_dim.56.weight_ref
  48.6 6.1 %legendre.1 = bf16[32,2,80,128]{3,2,1,0:T(8,128)(2,1)} custom-call(f32[1288,128]{1,0:T(8,128)S(1)} %broadcast_in_dim.56.weight_ref, bf16[32,2,80,128]{3,2,1,0:T(8,128)(2,1)S(1)} %bitcast.4, bf16[2,2,640,1280]{3,2,1,0:T(8,128)(2,1)} %table_hbm.1), custom_call_target="tpu_custom_call" | custom-call | tf_op jit(solution)/shard_map/legendre/pallas_call | solution.py:174
  54.7 6.4 %all-to-all-start.1 = ((bf16[64,80,128]{2,1,0:T(8,128)(2,1)}), bf16[64,80,128]{2,1,0:T(8,128)(2,1)S(1)}, u32[]{:S(2)}, u32[]{:S(2)}) async-start(bf16[64,80,128]{2,1,0:T(8,128)(2,1)} %bitcast.2), calls=%async_computation.1 | async-start | bytes 2621440 | tf_op jit(solution)/shard_map/all_to_all | solution.py:359
  61.1 0.1 broadcast_in_dim.52
  61.2 0.1 broadcast_in_dim_reshape.5
  61.2 0.1 broadcast_in_dim_reshape.6
  61.4 0.1 fusion.7
  61.5 32.2 %all-to-all-done.1.x_ref = bf16[64,80,128]{2,1,0:T(8,128)(2,1)S(1)} async-done(((bf16[64,80,128]{2,1,0:T(8,128)(2,1)}), bf16[64,80,128]{2,1,0:T(8,128)(2,1)S(1)}, u32[]{:S(2)}, u32[]{:S(2)}) %all-to-all-start.1) | async-done | bytes 1310752 | tf_op jit(solution)/shard_map/all_to_all | solution.py:359
  93.7 1.4 %totals.1 = f32[80,128]{1,0:T(8,128)S(1)} custom-call(s32[64]{0:T(128)S(1)} %copy-done, bf16[8,128]{1,0:T(8,128)(2,1)S(1)} %concatenate.39.sum_ref, bf16[64,80,128]{2,1,0:T(8,128)(2,1)S(1)} %all-to-all-done.1.x_ref), custom_call_target="tpu_custom_call" | custom-call | tf_op jit(solution)/shard_map/totals/pallas_call | solution.py:205
  95.1 0.1 collective-permute-start
  95.2 1.2 %collective-permute-done.own_ref = f32[80,128]{1,0:T(8,128)S(1)} collective-permute-done((f32[80,128]{1,0:T(8,128)S(1)}, f32[80,128]{1,0:T(8,128)S(1)}, u32[]{:S(2)}, u32[]{:S(2)}) %collective-permute-start) | collective-permute-done | bytes 40992 | tf_op jit(solution)/shard_map/ppermute | solution.py:330
  96.4 2.8 %collective-permute-start.1 = (f32[80,128]{1,0:T(8,128)S(1)}, f32[80,128]{1,0:T(8,128)S(1)}, u32[]{:S(2)}, u32[]{:S(2)}) collective-permute-start(f32[80,128]{1,0:T(8,128)S(1)} %add.59), channel_id=1, source_target_pairs={{0,6},{1,7},{2,0},{3,1},{4,2},{5,3},{6,4},{7,5},{8,14},{9,15},{10,... | collective-permute-start | bytes 122888 | tf_op jit(solution)/shard_map/ppermute | solution.py:333
  99.2 0.8 collective-permute-start.2
  100.0 0.9 collective-permute-start.3
  100.9 0.1 fusion.2.mix_ref
  100.9 2.7 %unpack.1 = (bf16[80,64,128]{2,1,0:T(8,128)(2,1)}, f32[80,16,128]{2,1,0:T(8,128)S(1)}) custom-call(s32[64]{0:T(128)S(1)} %copy-done, bf16[192,128]{1,0:T(8,128)(2,1)S(1)} %fusion.2.mix_ref, bf16[64,80,128]{2,1,0:T(8,128)(2,1)S(1)} %all-to-all-done.1.x_ref), custom_call_target="tpu_custom_call" | custom-call | tf_op jit(solution)/shard_map/unpack/pallas_call | solution.py:253
  103.7 1.0 collective-permute-done.2.refs_1_
  104.7 0.5 collective-permute-done.3.refs_2_
  105.2 0.8 finish.1
  (20 shorter events, 0.1 us)
Async XLA Ops:
  3.7 11.8 %copy-start = (s32[64]{0:T(128)S(1)}, s32[64]{0:T(128)}, u32[]{:S(2)}) copy-start(s32[64]{0:T(128)} %owner_ref.3) | copy-start | bytes 772
  3.7 12.0 %copy-start.1 = (f32[1280]{0:T(1024)S(1)}, f32[1280]{0:T(1024)}, u32[]{:S(2)}) copy-start(f32[1280]{0:T(1024)} %param.8) | copy-start | bytes 15364
  3.8 44.6 %all-to-all-start = ((bf16[64,80,128]{2,1,0:T(8,128)(2,1)}), bf16[64,80,128]{2,1,0:T(8,128)(2,1)S(1)}, u32[]{:S(2)}, u32[]{:S(2)}) async-start(bf16[64,80,128]{2,1,0:T(8,128)(2,1)} %pack.1), calls=%async_computation | async-start | bytes 2621440 | tf_op jit(solution)/shard_map/all_to_all | solution.py:355
  54.7 6.4 %copy-start.2 = (f32[16]{0:T(128)S(1)}, f32[16]{0:T(128)}, u32[]{:S(2)}) copy-start(f32[16]{0:T(128)} %param.9) | copy-start | bytes 196
  54.7 39.0 %all-to-all-start.1 = ((bf16[64,80,128]{2,1,0:T(8,128)(2,1)}), bf16[64,80,128]{2,1,0:T(8,128)(2,1)S(1)}, u32[]{:S(2)}, u32[]{:S(2)}) async-start(bf16[64,80,128]{2,1,0:T(8,128)(2,1)} %bitcast.2), calls=%async_computation.1 | async-start | bytes 2621440 | tf_op jit(solution)/shard_map/all_to_all | solution.py:359
  95.1 1.3 %collective-permute-start = (f32[80,128]{1,0:T(8,128)S(1)}, f32[80,128]{1,0:T(8,128)S(1)}, u32[]{:S(2)}, u32[]{:S(2)}) collective-permute-start(f32[80,128]{1,0:T(8,128)S(1)} %totals.1), channel_id=1, source_target_pairs={{0,1},{1,0},{2,3},{3,2},{4,5},{5,4},{6,7},{7,6},{8,9},{9,8},{10,11... | collective-permute-start | bytes 122888 | tf_op jit(solution)/shard_map/ppermute | solution.py:330
  96.4 7.3 %collective-permute-start.1 = (f32[80,128]{1,0:T(8,128)S(1)}, f32[80,128]{1,0:T(8,128)S(1)}, u32[]{:S(2)}, u32[]{:S(2)}) collective-permute-start(f32[80,128]{1,0:T(8,128)S(1)} %add.59), channel_id=1, source_target_pairs={{0,6},{1,7},{2,0},{3,1},{4,2},{5,3},{6,4},{7,5},{8,14},{9,15},{10,... | collective-permute-start | bytes 122888 | tf_op jit(solution)/shard_map/ppermute | solution.py:333
  99.2 5.5 %collective-permute-start.2 = (f32[80,128]{1,0:T(8,128)S(1)}, f32[80,128]{1,0:T(8,128)S(1)}, u32[]{:S(2)}, u32[]{:S(2)}) collective-permute-start(f32[80,128]{1,0:T(8,128)S(1)} %add.59), channel_id=1, source_target_pairs={{0,4},{1,5},{2,6},{3,7},{4,0},{5,1},{6,2},{7,3},{8,12},{9,13},{10,... | collective-permute-start | bytes 122888 | tf_op jit(solution)/shard_map/ppermute | solution.py:333
  100.0 5.2 %collective-permute-start.3 = (f32[80,128]{1,0:T(8,128)S(1)}, f32[80,128]{1,0:T(8,128)S(1)}, u32[]{:S(2)}, u32[]{:S(2)}) collective-permute-start(f32[80,128]{1,0:T(8,128)S(1)} %add.59), channel_id=1, source_target_pairs={{0,2},{1,3},{2,4},{3,5},{4,6},{5,7},{6,0},{7,1},{8,10},{9,11},{10,... | collective-permute-start | bytes 122888 | tf_op jit(solution)/shard_map/ppermute | solution.py:333

commit v4 on v3

--- a/solution.py
+++ b/solution.py
@@ -188,29 +188,31 @@
     )(weight, x, table)
 
 
-def totals_kernel(owner_ref, sum_ref, x_ref, out_ref, lines):
+def totals_kernel(sum_ref, x_ref, out_ref):
     waves, lat_rows, lanes = x_ref.shape
     weight = sum_ref[...]
-    lines[...] = jnp.zeros_like(lines)
-    for wave in range(waves):
-        line = dot(weight, x_ref[owner_ref[wave]], NT)
-        line = line[0:2] + line[2:4]
-        lines[wave : wave + 1, :lat_rows] = line[0:1]
-        lines[waves + wave : waves + wave + 1, :lat_rows] = line[1:2]
-    out_ref[...] = lines[...].T[:lat_rows]
-
-
-def totals(x, owner, weight):
+    lane = lax.broadcasted_iota(jnp.int32, (lat_rows, lanes), 1) % waves
+    state = jnp.zeros((lat_rows, lanes), F32)
+    for first in range(0, waves, 8):
+        group = range(first, first + 8)
+        rows = jnp.concatenate([x_ref[wave] for wave in group], axis=0)
+        spread = dot(jnp.concatenate([rows, rows], axis=1), weight, NN)
+        for step, wave in enumerate(group):
+            side = spread[step * lat_rows : (step + 1) * lat_rows]
+            state = jnp.where(lane == wave, side, state)
+    out_ref[...] = state
+
+
+def totals(x, weight):
     waves, lat_rows, lanes = x.shape
     return pl.pallas_call(
         totals_kernel,
         out_shape=jax.ShapeDtypeStruct((lat_rows, lanes), F32),
-        in_specs=[SMEM, VMEM, VMEM],
+        in_specs=[VMEM, VMEM],
         out_specs=VMEM,
-        scratch_shapes=[pltpu.VMEM((lanes, lanes), F32)],
         name="totals",
         compiler_params=pltpu.CompilerParams(vmem_limit_bytes=6 * MIB),
-    )(owner, weight, x)
+    )(weight, x)
 
 
 def unpack_kernel(owner_ref, mix_ref, x_ref, out_hbm, geo_ref, out_ref, spread, sems):
@@ -268,7 +270,7 @@
     )(owner, mix, x)
 
 
-def finish_kernel(inside_ref, own_ref, *refs):
+def finish_kernel(order_ref, inside_ref, own_ref, *refs):
     *later_refs, out_ref, below = refs
     lat_rows = out_ref.shape[0]
     north = northern()
@@ -277,23 +279,27 @@
     for step, ref in enumerate(later_refs):
         ahead = lev // 2 + step + 1 <= len(later_refs)
         state = state + jnp.where(ahead, ref[...], 0.0)
-    below[...] = state
+    terms = []
+    for _ in range(3):
+        terms.append(state.astype(BF16))
+        state = state - terms[-1].astype(F32)
+    below[...] = sum(dot(term, order_ref[...], NN) for term in terms)
     for lat in range(lat_rows):
         place = jnp.where(north, lat, lat_rows - 1 - lat)
         out_ref[lat] = (inside_ref[lat] + below[pl.ds(place, 1), :]).astype(BF16)
 
 
-def finish(inside, other, later):
+def finish(order, inside, other, later):
     lat_rows, levels, lanes = inside.shape
     return pl.pallas_call(
         finish_kernel,
         out_shape=jax.ShapeDtypeStruct(inside.shape, BF16),
-        in_specs=[VMEM] * (2 + len(later)),
+        in_specs=[VMEM] * (3 + len(later)),
         out_specs=VMEM,
         scratch_shapes=[pltpu.VMEM((lat_rows, lanes), F32)],
         name="finish",
         compiler_params=pltpu.CompilerParams(vmem_limit_bytes=6 * MIB),
-    )(inside, other, *later)
+    )(order, inside, other, *later)
 
 
 def two_terms(weight):
@@ -317,11 +323,10 @@
     mix = jnp.concatenate(
         [jnp.concatenate(pair, axis=1) for pair in ((inside, blank), (blank, inside))], axis=0
     )
-    high, low = two_terms(depth)
-    blank = jnp.zeros_like(high)
-    pieces = ((high, blank), (blank, high), (low, blank), (blank, low))
-    every = [jnp.concatenate(piece, axis=1) for piece in pieces]
-    every = jnp.concatenate(every + [jnp.zeros((4, 2 * columns), BF16)], axis=0)
+    part = jnp.arange(2 * columns) // columns
+    same = part[:, None] == part[None, :]
+    every = jnp.where(same, jnp.tile(depth[0], 2)[:, None], 0.0)
+    every = jnp.concatenate(two_terms(every), axis=0)
     return mix, every
 
 
@@ -350,6 +355,8 @@
     lines = jnp.concatenate([quad_weights, lengths.astype(F32), jnp.zeros((8 - slots,), F32)])
     weight = jnp.broadcast_to(lines[:, None], (lines.shape[0], doubled))
     mix, every = level_sums(layer_depth, field_count)
+    both = jnp.concatenate([owner, owner + waves])
+    order = (both[None, :] == jnp.arange(doubled)[:, None]).astype(BF16)
 
     outgoing = pack(fourier, owner)
     arrived = lax.all_to_all(outgoing, "wave", split_axis=0, concat_axis=0, tiled=True)
@@ -357,10 +364,10 @@
     results = legendre_pair(arrived, legendre, weight)
     results = results.reshape(waves, lat_rows, doubled)
     returned = lax.all_to_all(results, "wave", split_axis=0, concat_axis=0, tiled=True)
-    other, later = sums_of_later(totals(returned, owner, every))
+    other, later = sums_of_later(totals(returned, every))
     fields, inside = unpack(returned, owner, mix, level_count)
     fields_out = fields.reshape(fourier.shape)
-    geopotential = finish(inside, other, later)
+    geopotential = finish(order, inside, other, later)
     return (fields_out, geopotential)
 
 

time: 106 us -> 106 us (level)
  no operation moved by 1% of the time
where the time goes in v4:
time: 106 us
  waiting for transfers between devices  67.4 us (64%)
  starting transfers between devices  22.6 us (21%)
  Pallas kernels  13.7 us (13%)
    all_to_all x1, waiting for transfers between devices, on_device(): lax.all_to_all(outgoing, 'wave', split_axis=0, concat_axis=0, tiled=True)  32.6 us
    all_to_all x1, waiting for transfers between devices, on_device(): lax.all_to_all(results, 'wave', split_axis=0, concat_axis=0, tiled=True)  32.1 us
    all_to_all x1, starting transfers between devices, on_device(): lax.all_to_all(outgoing, 'wave', split_axis=0, concat_axis=0, tiled=True)  11.7 us
    all_to_all x1, starting transfers between devices, on_device(): lax.all_to_all(results, 'wave', split_axis=0, concat_axis=0, tiled=True)  6.35 us
    pallas_call x1, Pallas kernels, legendre_pair(): pl.pallas_call(legendre_kernel, out_shape=jax.ShapeDtypeStruct(x.shape, B...  6.07 us
    ppermute x3, starting transfers between devices, sums_of_later(): lax.ppermute(both, 'lev', [(i, (i - step) % count) for i in range(count)])  4.44 us
    pallas_call x1, Pallas kernels, pack(): pl.pallas_call(pack_kernel, out_shape=jax.ShapeDtypeStruct((waves, lat_ro...  3.09 us
    pallas_call x1, Pallas kernels, unpack(): pl.pallas_call(unpack_kernel, out_shape=(jax.ShapeDtypeStruct((lat_rows,...  2.72 us
  transfers between devices with their start and end apart: 6, of which 5 were waited for; matrix products, arithmetic and copies ran while one was open for 1% of the time, Pallas kernels for 3%

profile of v4, /device:TPU:8, one launch (start us, length us, event | category | flops | bytes accessed | tf_op | source)
XLA Modules:
  0.0 105.6 jit_solution(10981288558417501740)
XLA Ops:
  0.6 3.1 %pack.1 = bf16[64,80,128]{2,1,0:T(8,128)(2,1)} custom-call(s32[64]{0:T(128)} %owner_ref.1, bf16[5120,128]{1,0:T(8,128)(2,1)} %bitcast.5), custom_call_target="tpu_custom_call" | custom-call | tf_op jit(solution)/shard_map/pack/pallas_call | solution.py:97
  3.8 11.7 %all-to-all-start = ((bf16[64,80,128]{2,1,0:T(8,128)(2,1)}), bf16[64,80,128]{2,1,0:T(8,128)(2,1)S(1)}, u32[]{:S(2)}, u32[]{:S(2)}) async-start(bf16[64,80,128]{2,1,0:T(8,128)(2,1)} %pack.1), calls=%async_computation | async-start | bytes 2621440 | tf_op jit(solution)/shard_map/all_to_all | solution.py:362
  15.5 0.2 fusion.7
  15.7 0.1 concatenate.25
  15.8 32.6 %all-to-all-done = bf16[64,80,128]{2,1,0:T(8,128)(2,1)S(1)} async-done(((bf16[64,80,128]{2,1,0:T(8,128)(2,1)}), bf16[64,80,128]{2,1,0:T(8,128)(2,1)S(1)}, u32[]{:S(2)}, u32[]{:S(2)}) %all-to-all-start) | async-done | bytes 1310752 | tf_op jit(solution)/shard_map/all_to_all | solution.py:362
  48.4 0.2 broadcast_in_dim.68.weight_ref
  48.6 6.1 %legendre.1 = bf16[32,2,80,128]{3,2,1,0:T(8,128)(2,1)} custom-call(f32[1288,128]{1,0:T(8,128)S(1)} %broadcast_in_dim.68.weight_ref, bf16[32,2,80,128]{3,2,1,0:T(8,128)(2,1)S(1)} %bitcast.4, bf16[2,2,640,1280]{3,2,1,0:T(8,128)(2,1)} %table_hbm.1), custom_call_target="tpu_custom_call" | custom-call | tf_op jit(solution)/shard_map/legendre/pallas_call | solution.py:174
  54.7 6.4 %all-to-all-start.1 = ((bf16[64,80,128]{2,1,0:T(8,128)(2,1)}), bf16[64,80,128]{2,1,0:T(8,128)(2,1)S(1)}, u32[]{:S(2)}, u32[]{:S(2)}) async-start(bf16[64,80,128]{2,1,0:T(8,128)(2,1)} %bitcast.2), calls=%async_computation.1 | async-start | bytes 2621440 | tf_op jit(solution)/shard_map/all_to_all | solution.py:366
  61.1 0.1 broadcast_in_dim_reshape.3
  61.3 0.1 broadcast_in_dim.69
  61.3 0.1 pad_add_fusion
  61.4 0.1 reduce-precision_convert_fusion
  61.6 32.1 %all-to-all-done.1.x_ref = bf16[64,80,128]{2,1,0:T(8,128)(2,1)S(1)} async-done(((bf16[64,80,128]{2,1,0:T(8,128)(2,1)}), bf16[64,80,128]{2,1,0:T(8,128)(2,1)S(1)}, u32[]{:S(2)}, u32[]{:S(2)}) %all-to-all-start.1) | async-done | bytes 1310752 | tf_op jit(solution)/shard_map/all_to_all | solution.py:366
  93.7 0.8 totals.1
  94.5 0.1 collective-permute-start
  94.7 1.2 %collective-permute-done.own_ref = f32[80,128]{1,0:T(8,128)S(1)} collective-permute-done((f32[80,128]{1,0:T(8,128)S(1)}, f32[80,128]{1,0:T(8,128)S(1)}, u32[]{:S(2)}, u32[]{:S(2)}) %collective-permute-start) | collective-permute-done | bytes 40992 | tf_op jit(solution)/shard_map/ppermute | solution.py:335
  95.9 2.8 %collective-permute-start.1 = (f32[80,128]{1,0:T(8,128)S(1)}, f32[80,128]{1,0:T(8,128)S(1)}, u32[]{:S(2)}, u32[]{:S(2)}) collective-permute-start(f32[80,128]{1,0:T(8,128)S(1)} %add.55), channel_id=1, source_target_pairs={{0,6},{1,7},{2,0},{3,1},{4,2},{5,3},{6,4},{7,5},{8,14},{9,15},{10,... | collective-permute-start | bytes 122888 | tf_op jit(solution)/shard_map/ppermute | solution.py:338
  98.6 0.8 collective-permute-start.2
  99.4 0.9 collective-permute-start.3
  100.3 0.1 fusion.4.mix_ref
  100.4 2.7 %unpack.1 = (bf16[80,64,128]{2,1,0:T(8,128)(2,1)}, f32[80,16,128]{2,1,0:T(8,128)S(1)}) custom-call(s32[64]{0:T(128)S(1)} %copy-done, bf16[192,128]{1,0:T(8,128)(2,1)S(1)} %fusion.4.mix_ref, bf16[64,80,128]{2,1,0:T(8,128)(2,1)S(1)} %all-to-all-done.1.x_ref), custom_call_target="tpu_custom_call" | custom-call | tf_op jit(solution)/shard_map/unpack/pallas_call | solution.py:255
  103.1 1.0 collective-permute-done.2.refs_1_
  104.1 0.5 collective-permute-done.3.refs_2_
  104.6 1.0 finish.1
  (22 shorter events, 0.2 us)
Async XLA Ops:
  3.7 11.8 %copy-start = (s32[64]{0:T(128)S(1)}, s32[64]{0:T(128)}, u32[]{:S(2)}) copy-start(s32[64]{0:T(128)} %owner_ref.1) | copy-start | bytes 772
  3.7 12.0 %copy-start.1 = (f32[1280]{0:T(1024)S(1)}, f32[1280]{0:T(1024)}, u32[]{:S(2)}) copy-start(f32[1280]{0:T(1024)} %param.8) | copy-start | bytes 15364
  3.8 44.6 %all-to-all-start = ((bf16[64,80,128]{2,1,0:T(8,128)(2,1)}), bf16[64,80,128]{2,1,0:T(8,128)(2,1)S(1)}, u32[]{:S(2)}, u32[]{:S(2)}) async-start(bf16[64,80,128]{2,1,0:T(8,128)(2,1)} %pack.1), calls=%async_computation | async-start | bytes 2621440 | tf_op jit(solution)/shard_map/all_to_all | solution.py:362
  54.7 6.4 %copy-start.2 = (f32[16]{0:T(128)S(1)}, f32[16]{0:T(128)}, u32[]{:S(2)}) copy-start(f32[16]{0:T(128)} %param.9) | copy-start | bytes 196
  54.7 39.0 %all-to-all-start.1 = ((bf16[64,80,128]{2,1,0:T(8,128)(2,1)}), bf16[64,80,128]{2,1,0:T(8,128)(2,1)S(1)}, u32[]{:S(2)}, u32[]{:S(2)}) async-start(bf16[64,80,128]{2,1,0:T(8,128)(2,1)} %bitcast.2), calls=%async_computation.1 | async-start | bytes 2621440 | tf_op jit(solution)/shard_map/all_to_all | solution.py:366
  94.5 1.3 %collective-permute-start = (f32[80,128]{1,0:T(8,128)S(1)}, f32[80,128]{1,0:T(8,128)S(1)}, u32[]{:S(2)}, u32[]{:S(2)}) collective-permute-start(f32[80,128]{1,0:T(8,128)S(1)} %totals.1), channel_id=1, source_target_pairs={{0,1},{1,0},{2,3},{3,2},{4,5},{5,4},{6,7},{7,6},{8,9},{9,8},{10,11... | collective-permute-start | bytes 122888 | tf_op jit(solution)/shard_map/ppermute | solution.py:335
  95.9 7.2 %collective-permute-start.1 = (f32[80,128]{1,0:T(8,128)S(1)}, f32[80,128]{1,0:T(8,128)S(1)}, u32[]{:S(2)}, u32[]{:S(2)}) collective-permute-start(f32[80,128]{1,0:T(8,128)S(1)} %add.55), channel_id=1, source_target_pairs={{0,6},{1,7},{2,0},{3,1},{4,2},{5,3},{6,4},{7,5},{8,14},{9,15},{10,... | collective-permute-start | bytes 122888 | tf_op jit(solution)/shard_map/ppermute | solution.py:338
  98.6 5.5 %collective-permute-start.2 = (f32[80,128]{1,0:T(8,128)S(1)}, f32[80,128]{1,0:T(8,128)S(1)}, u32[]{:S(2)}, u32[]{:S(2)}) collective-permute-start(f32[80,128]{1,0:T(8,128)S(1)} %add.55), channel_id=1, source_target_pairs={{0,4},{1,5},{2,6},{3,7},{4,0},{5,1},{6,2},{7,3},{8,12},{9,13},{10,... | collective-permute-start | bytes 122888 | tf_op jit(solution)/shard_map/ppermute | solution.py:338
  99.4 5.2 %collective-permute-start.3 = (f32[80,128]{1,0:T(8,128)S(1)}, f32[80,128]{1,0:T(8,128)S(1)}, u32[]{:S(2)}, u32[]{:S(2)}) collective-permute-start(f32[80,128]{1,0:T(8,128)S(1)} %add.55), channel_id=1, source_target_pairs={{0,2},{1,3},{2,4},{3,5},{4,6},{5,7},{6,0},{7,1},{8,10},{9,11},{10,... | collective-permute-start | bytes 122888 | tf_op jit(solution)/shard_map/ppermute | solution.py:338
